TPU v7x, 256 devices: a whole 4x4x8 slice. The times are simulated.
256 devices in a mesh: gx: 32 (over y_lo, z, core), gy: 8 (over y_hi, x).
Axes of the slice: x: 4, y: 4 (y_hi: 2, y_lo: 2; y = y_hi * 2 + y_lo), z: 8, core: 2. Of those that a mesh axis runs over, the one named last changes fastest.
Arguments:
- input_one: float32 [32, 2, 128, 1024], P(None, None, 'gx', 'gy'), may hold values from -6 to 6
- input_two: float32 [32, 2, 128, 1024], P(None, None, 'gx', 'gy'), may hold values from -6 to 6
- input_three: float32 [32, 2, 128, 1024], P(None, None, 'gx', 'gy'), may hold values from -6 to 6
- cotangent: float32 [32, 2, 128, 1024], P(None, None, 'gx', 'gy'), may hold values from -6 to 6
- kernel_one: float32 [27, 32, 32], replicated, may hold values from -0.21875 to 0.21875
- kernel_two: float32 [27, 32, 32], replicated, may hold values from -0.21875 to 0.21875
- kernel_three: float32 [27, 32, 32], replicated, may hold values from -0.21875 to 0.21875
Outputs:
- grad_input: float32 [32, 2, 128, 1024], P(None, None, 'gx', 'gy')
- grad_kernel_one: float32 [27, 32, 32], replicated
- grad_kernel_two: float32 [27, 32, 32], replicated
- grad_kernel_three: float32 [27, 32, 32], replicated
All inputs are finite; a program needn't handle non-finite values.
Results may differ from a plain program's by a relative error of at most 0.00013.
Values sent between devices are 32-bit elements; how exact they have to be, the bound alone decides.
A program may use at most 64 MiB of HBM per device.

v0:
```python
import math

import jax
import jax.numpy as jnp
from jax import lax
from jax.sharding import PartitionSpec as P

inv_root_two = 0.7071067811865476
inv_root_two_pi = 0.3989422804014327


def with_halo(value, sides, width):
    for axis, dim in sides:
        size, length = (lax.axis_size(axis), value.shape[dim])
        up = [(i, (i + 1) % size) for i in range(size - 1)]
        down = [(j, i) for i, j in up]
        last = lax.slice_in_dim(value, length - width, length, axis=dim)
        leading = lax.slice_in_dim(value, 0, width, axis=dim)
        before = lax.ppermute(last, axis, up)
        after = lax.ppermute(leading, axis, down)
        value = jnp.concatenate([before, value, after], axis=dim)
    return value


def gelu_slope(value):
    normal_cdf = 0.5 * (1.0 + jax.scipy.special.erf(value * inv_root_two))
    density = jnp.exp(-0.5 * value * value) * inv_root_two_pi
    return normal_cdf + value * density


def conv_taps(padded, kernel, depth, rows, cols):
    total = None
    for tap in range(27):
        a, b, c = (tap // 9, tap // 3 % 3, tap % 3)
        window = padded[:, a : a + depth, b : b + rows, c : c + cols]
        term = jnp.einsum("oi,izxy->ozxy", kernel[tap], window, precision=lax.Precision.HIGHEST)
        total = term if total is None else total + term
    return total


def back_taps(padded, kernel, depth, rows, cols):
    total = None
    for tap in range(27):
        a, b, c = (tap // 9, tap // 3 % 3, tap % 3)
        window = padded[:, 2 - a : 2 - a + depth, 2 - b : 2 - b + rows, 2 - c : 2 - c + cols]
        term = jnp.einsum("oi,ozxy->izxy", kernel[tap], window, precision=lax.Precision.HIGHEST)
        total = term if total is None else total + term
    return total


def kernel_terms(padded, slope_grad, depth, rows, cols):
    parts = []
    for tap in range(27):
        a, b, c = (tap // 9, tap // 3 % 3, tap % 3)
        window = padded[:, a : a + depth, b : b + rows, c : c + cols]
        parts.append(
            jnp.einsum("ozxy,izxy->oi", slope_grad, window, precision=lax.Precision.HIGHEST)
        )
    return jnp.stack(parts, axis=0)


def depth_pad(field):
    return jnp.pad(field, ((0, 0), (1, 1), (0, 0), (0, 0)))


def per_device(input_one, input_two, input_three, cotangent, kernel_one, kernel_two, kernel_three):
    depth, rows, cols = (input_one.shape[1], input_one.shape[2], input_one.shape[3])
    factor = 1.0 / math.sqrt(depth * rows * cols * lax.axis_size("gx") * lax.axis_size("gy"))
    fields = (input_three, input_two, input_one)
    kernels = (kernel_three, kernel_two, kernel_one)
    grad = cotangent
    results = []
    for layer in range(3):
        kernel = kernels[layer]
        padded = depth_pad(with_halo(fields[layer], (("gx", 2), ("gy", 3)), 1))
        pre = conv_taps(padded, kernel, depth, rows, cols)
        slope_grad = grad * gelu_slope(pre)
        terms = kernel_terms(padded, slope_grad, depth, rows, cols)
        results.append(lax.psum(terms, ("gx", "gy")) * factor)
        grad_padded = depth_pad(with_halo(slope_grad, (("gx", 2), ("gy", 3)), 1))
        grad = back_taps(grad_padded, kernel, depth, rows, cols)
    return (grad, results[2], results[1], results[0])


def solution(mesh):
    placed = (
        P(None, None, "gx", "gy"),
        P(None, None, "gx", "gy"),
        P(None, None, "gx", "gy"),
        P(None, None, "gx", "gy"),
        P(),
        P(),
        P(),
    )
    return jax.shard_map(
        per_device,
        mesh=mesh,
        in_specs=placed,
        out_specs=(P(None, None, "gx", "gy"), P(), P(), P()),
        check_vma=False,
    )
```

profile of v0, /device:TPU:1, one launch (start us, length us, event | category | flops | bytes accessed | tf_op | source)
XLA Modules:
  0.0 450.1 jit_solution(10008762953945077907)
XLA Ops:
  8.3 4.9 %collective-permute-start = (f32[32,2,1,128]{3,0,2,1:T(8,128)S(1)}, f32[32,2,1,128]{3,0,2,1:T(8,128)S(1)}, u32[]{:S(2)}, u32[]{:S(2)}) collective-permute-start(f32[32,2,1,128]{3,0,2,1:T(8,128)S(1)} %copy.938), channel_id=1, source_target_pairs={{0,8},{8,16},{16,24},{24,32},{32,40},{40,48},{48,56},{56,64},{64,7... | collective-permute-start | bytes 98312 | tf_op jit(solution)/shard_map/ppermute | solution.py:19
  13.2 2.1 collective-permute-start.1
  15.4 3.6 collective-permute-start.8
  19.1 1.9 collective-permute-start.9
  21.1 3.8 collective-permute-start.16
  24.9 1.9 collective-permute-start.17
  27.0 3.1 collective-permute-start.2
  32.2 4.0 collective-permute-start.10
  38.3 4.0 collective-permute-start.18
  68.7 5.0 %collective-permute-start.4 = (f32[32,2,1,128]{3,0,2,1:T(8,128)S(1)}, f32[32,2,1,128]{3,0,2,1:T(8,128)S(1)}, u32[]{:S(2)}, u32[]{:S(2)}) collective-permute-start(f32[32,2,1,128]{3,0,2,1:T(8,128)S(1)} %get-tuple-element.124), channel_id=1, source_target_pairs={{0,8},{8,16},{16,24},{24,32},{32,40},{40,48},{48,56},{56,64},{64,7... | collective-permute-start | bytes 98312 | tf_op jit(solution)/shard_map/ppermute | solution.py:19
  73.8 1.9 collective-permute-start.5
  86.1 4.3 collective-permute-start.6
  90.3 1.7 collective-permute-start.7
  92.9 7.5 %collective-permute-done.7 = f32[32,2,6,1]{3,0,2,1:T(8,128)S(1)} collective-permute-done((f32[32,2,6,1]{3,0,2,1:T(8,128)S(1)}, f32[32,2,6,1]{3,0,2,1:T(8,128)S(1)}, u32[]{:S(2)}, u32[]{:S(2)}) %collective-permute-start.7) | collective-permute-done | bytes 1568 | tf_op jit(solution)/shard_map/ppermute | solution.py:20
  114.1 6.3 %collective-permute-start.12 = (f32[32,2,1,128]{3,0,2,1:T(8,128)S(1)}, f32[32,2,1,128]{3,0,2,1:T(8,128)S(1)}, u32[]{:S(2)}, u32[]{:S(2)}) collective-permute-start(f32[32,2,1,128]{3,0,2,1:T(8,128)S(1)} %get-tuple-element.117), channel_id=1, source_target_pairs={{0,8},{8,16},{16,24},{24,32},{32,40},{40,48},{48,56},{56,64},{64,7... | collective-permute-start | bytes 98312 | tf_op jit(solution)/shard_map/ppermute | solution.py:19
  120.4 1.9 collective-permute-start.13
  125.8 7.3 %collective-permute-start.14 = (f32[32,2,6,1]{3,0,2,1:T(8,128)S(1)}, f32[32,2,6,1]{3,0,2,1:T(8,128)S(1)}, u32[]{:S(2)}, u32[]{:S(2)}) collective-permute-start(f32[32,2,6,1]{3,0,2,1:T(8,128)S(1)} %get-tuple-element.95), channel_id=1, source_target_pairs={{0,1},{1,2},{2,3},{3,4},{4,5},{5,6},{6,7},{8,9},{9,10},{10,11},{11... | collective-permute-start | bytes 4616 | tf_op jit(solution)/shard_map/ppermute | solution.py:19
  136.1 7.7 %collective-permute-done.15 = f32[32,2,6,1]{3,0,2,1:T(8,128)S(1)} collective-permute-done((f32[32,2,6,1]{3,0,2,1:T(8,128)S(1)}, f32[32,2,6,1]{3,0,2,1:T(8,128)S(1)}, u32[]{:S(2)}, u32[]{:S(2)}) %collective-permute-start.15) | collective-permute-done | bytes 1568 | tf_op jit(solution)/shard_map/ppermute | solution.py:20
  157.5 6.0 %collective-permute-start.20 = (f32[32,2,1,128]{3,0,2,1:T(8,128)S(1)}, f32[32,2,1,128]{3,0,2,1:T(8,128)S(1)}, u32[]{:S(2)}, u32[]{:S(2)}) collective-permute-start(f32[32,2,1,128]{3,0,2,1:T(8,128)S(1)} %get-tuple-element.110), channel_id=1, source_target_pairs={{0,8},{8,16},{16,24},{24,32},{32,40},{40,48},{48,56},{56,64},{64,7... | collective-permute-start | bytes 98312 | tf_op jit(solution)/shard_map/ppermute | solution.py:19
  163.4 1.9 collective-permute-start.21
  168.8 6.4 %collective-permute-start.22 = (f32[32,2,6,1]{3,0,2,1:T(8,128)S(1)}, f32[32,2,6,1]{3,0,2,1:T(8,128)S(1)}, u32[]{:S(2)}, u32[]{:S(2)}) collective-permute-start(f32[32,2,6,1]{3,0,2,1:T(8,128)S(1)} %get-tuple-element.86), channel_id=1, source_target_pairs={{0,1},{1,2},{2,3},{3,4},{4,5},{5,6},{6,7},{8,9},{9,10},{10,11},{11... | collective-permute-start | bytes 4616 | tf_op jit(solution)/shard_map/ppermute | solution.py:19
  178.3 4.4 collective-permute-done.23
  192.3 247.8 %all-reduce.9.cloned.1.call-done = (f32[27,32,32]{2,1,0:T(8,128)}, f32[27,32,32]{2,1,0:T(8,128)}, f32[27,32,32]{2,1,0:T(8,128)}) async-done(((f32[27,32,32]{2,1,0:T(8,128)}, f32[27,32,32]{2,1,0:T(8,128)}, f32[27,32,32]{2,1,0:T(8,128)}), (f32[27,32,32]{2,1,0:T(8,128)}, f32[27,32,32]{2,1,0:T(8,128)}, f32[27,32,32]{2,1,0:T(8,128)})) %all-reduce.9.cloned.1.call-update) | async-done | bytes 331792 | tf_op jit(solution)/shard_map/psum | solution.py:79
  440.1 1.9 broadcast_multiply_fusion.2
  (342 shorter events, 91.7 us)
Async XLA Ops:
  7.2 432.9 %all-reduce.9.cloned.1.call-start = ((), (), s32[]{:S(2)}) async-start(), calls=%async_computation | async-start | bytes 2654208 | tf_op jit(solution)/shard_map/psum | solution.py:79
  8.3 16.6 %collective-permute-start = (f32[32,2,1,128]{3,0,2,1:T(8,128)S(1)}, f32[32,2,1,128]{3,0,2,1:T(8,128)S(1)}, u32[]{:S(2)}, u32[]{:S(2)}) collective-permute-start(f32[32,2,1,128]{3,0,2,1:T(8,128)S(1)} %copy.938), channel_id=1, source_target_pairs={{0,8},{8,16},{16,24},{24,32},{32,40},{40,48},{48,56},{56,64},{64,7... | collective-permute-start | bytes 98312 | tf_op jit(solution)/shard_map/ppermute | solution.py:19
  13.2 13.6 %collective-permute-start.1 = (f32[32,2,1,128]{3,0,2,1:T(8,128)S(1)}, f32[32,2,1,128]{3,0,2,1:T(8,128)S(1)}, u32[]{:S(2)}, u32[]{:S(2)}) collective-permute-start(f32[32,2,1,128]{3,0,2,1:T(8,128)S(1)} %copy.939), channel_id=1, source_target_pairs={{8,0},{16,8},{24,16},{32,24},{40,32},{48,40},{56,48},{64,56},{72,6... | collective-permute-start | bytes 98312 | tf_op jit(solution)/shard_map/ppermute | solution.py:20
  15.4 15.0 %collective-permute-start.8 = (f32[32,2,1,128]{3,0,2,1:T(8,128)S(1)}, f32[32,2,1,128]{3,0,2,1:T(8,128)S(1)}, u32[]{:S(2)}, u32[]{:S(2)}) collective-permute-start(f32[32,2,1,128]{3,0,2,1:T(8,128)S(1)} %copy.940), channel_id=1, source_target_pairs={{0,8},{8,16},{16,24},{24,32},{32,40},{40,48},{48,56},{56,64},{64,7... | collective-permute-start | bytes 98312 | tf_op jit(solution)/shard_map/ppermute | solution.py:19
  19.1 13.0 %collective-permute-start.9 = (f32[32,2,1,128]{3,0,2,1:T(8,128)S(1)}, f32[32,2,1,128]{3,0,2,1:T(8,128)S(1)}, u32[]{:S(2)}, u32[]{:S(2)}) collective-permute-start(f32[32,2,1,128]{3,0,2,1:T(8,128)S(1)} %copy.941), channel_id=1, source_target_pairs={{8,0},{16,8},{24,16},{32,24},{40,32},{48,40},{56,48},{64,56},{72,6... | collective-permute-start | bytes 98312 | tf_op jit(solution)/shard_map/ppermute | solution.py:20
  21.1 15.4 %collective-permute-start.16 = (f32[32,2,1,128]{3,0,2,1:T(8,128)S(1)}, f32[32,2,1,128]{3,0,2,1:T(8,128)S(1)}, u32[]{:S(2)}, u32[]{:S(2)}) collective-permute-start(f32[32,2,1,128]{3,0,2,1:T(8,128)S(1)} %copy.942), channel_id=1, source_target_pairs={{0,8},{8,16},{16,24},{24,32},{32,40},{40,48},{48,56},{56,64},{64,7... | collective-permute-start | bytes 98312 | tf_op jit(solution)/shard_map/ppermute | solution.py:19
  24.9 13.2 %collective-permute-start.17 = (f32[32,2,1,128]{3,0,2,1:T(8,128)S(1)}, f32[32,2,1,128]{3,0,2,1:T(8,128)S(1)}, u32[]{:S(2)}, u32[]{:S(2)}) collective-permute-start(f32[32,2,1,128]{3,0,2,1:T(8,128)S(1)} %copy.943), channel_id=1, source_target_pairs={{8,0},{16,8},{24,16},{32,24},{40,32},{48,40},{56,48},{64,56},{72,6... | collective-permute-start | bytes 98312 | tf_op jit(solution)/shard_map/ppermute | solution.py:20
  27.0 15.7 %collective-permute-start.2 = (f32[32,2,6,1]{3,0,2,1:T(8,128)S(1)}, f32[32,2,6,1]{3,0,2,1:T(8,128)S(1)}, u32[]{:S(2)}, u32[]{:S(2)}) collective-permute-start(f32[32,2,6,1]{3,0,2,1:T(8,128)S(1)} %get-tuple-element.108), channel_id=1, source_target_pairs={{0,1},{1,2},{2,3},{3,4},{4,5},{5,6},{6,7},{8,9},{9,10},{10,11},{11... | collective-permute-start | bytes 4616 | tf_op jit(solution)/shard_map/ppermute | solution.py:19
  30.4 13.8 %collective-permute-start.3 = (f32[32,2,6,1]{3,0,2,1:T(8,128)S(1)}, f32[32,2,6,1]{3,0,2,1:T(8,128)S(1)}, u32[]{:S(2)}, u32[]{:S(2)}) collective-permute-start(f32[32,2,6,1]{3,0,2,1:T(8,128)S(1)} %get-tuple-element.109), channel_id=1, source_target_pairs={{1,0},{2,1},{3,2},{4,3},{5,4},{6,5},{7,6},{9,8},{10,9},{11,10},{12... | collective-permute-start | bytes 4616 | tf_op jit(solution)/shard_map/ppermute | solution.py:20
  32.2 13.4 %collective-permute-start.10 = (f32[32,2,6,1]{3,0,2,1:T(8,128)S(1)}, f32[32,2,6,1]{3,0,2,1:T(8,128)S(1)}, u32[]{:S(2)}, u32[]{:S(2)}) collective-permute-start(f32[32,2,6,1]{3,0,2,1:T(8,128)S(1)} %get-tuple-element.99), channel_id=1, source_target_pairs={{0,1},{1,2},{2,3},{3,4},{4,5},{5,6},{6,7},{8,9},{9,10},{10,11},{11... | collective-permute-start | bytes 4616 | tf_op jit(solution)/shard_map/ppermute | solution.py:19
  36.5 9.1 %collective-permute-start.11 = (f32[32,2,6,1]{3,0,2,1:T(8,128)S(1)}, f32[32,2,6,1]{3,0,2,1:T(8,128)S(1)}, u32[]{:S(2)}, u32[]{:S(2)}) collective-permute-start(f32[32,2,6,1]{3,0,2,1:T(8,128)S(1)} %get-tuple-element.100), channel_id=1, source_target_pairs={{1,0},{2,1},{3,2},{4,3},{5,4},{6,5},{7,6},{9,8},{10,9},{11,10},{12... | collective-permute-start | bytes 4616 | tf_op jit(solution)/shard_map/ppermute | solution.py:20
  38.3 17.0 %collective-permute-start.18 = (f32[32,2,6,1]{3,0,2,1:T(8,128)S(1)}, f32[32,2,6,1]{3,0,2,1:T(8,128)S(1)}, u32[]{:S(2)}, u32[]{:S(2)}) collective-permute-start(f32[32,2,6,1]{3,0,2,1:T(8,128)S(1)} %get-tuple-element.90), channel_id=1, source_target_pairs={{0,1},{1,2},{2,3},{3,4},{4,5},{5,6},{6,7},{8,9},{9,10},{10,11},{11... | collective-permute-start | bytes 4616 | tf_op jit(solution)/shard_map/ppermute | solution.py:19
  42.8 12.5 %collective-permute-start.19 = (f32[32,2,6,1]{3,0,2,1:T(8,128)S(1)}, f32[32,2,6,1]{3,0,2,1:T(8,128)S(1)}, u32[]{:S(2)}, u32[]{:S(2)}) collective-permute-start(f32[32,2,6,1]{3,0,2,1:T(8,128)S(1)} %get-tuple-element.91), channel_id=1, source_target_pairs={{1,0},{2,1},{3,2},{4,3},{5,4},{6,5},{7,6},{9,8},{10,9},{11,10},{12... | collective-permute-start | bytes 4616 | tf_op jit(solution)/shard_map/ppermute | solution.py:20
  68.7 16.6 %collective-permute-start.4 = (f32[32,2,1,128]{3,0,2,1:T(8,128)S(1)}, f32[32,2,1,128]{3,0,2,1:T(8,128)S(1)}, u32[]{:S(2)}, u32[]{:S(2)}) collective-permute-start(f32[32,2,1,128]{3,0,2,1:T(8,128)S(1)} %get-tuple-element.124), channel_id=1, source_target_pairs={{0,8},{8,16},{16,24},{24,32},{32,40},{40,48},{48,56},{56,64},{64,7... | collective-permute-start | bytes 98312 | tf_op jit(solution)/shard_map/ppermute | solution.py:19
  73.8 11.5 %collective-permute-start.5 = (f32[32,2,1,128]{3,0,2,1:T(8,128)S(1)}, f32[32,2,1,128]{3,0,2,1:T(8,128)S(1)}, u32[]{:S(2)}, u32[]{:S(2)}) collective-permute-start(f32[32,2,1,128]{3,0,2,1:T(8,128)S(1)} %get-tuple-element.125), channel_id=1, source_target_pairs={{8,0},{16,8},{24,16},{32,24},{40,32},{48,40},{56,48},{64,56},{72,6... | collective-permute-start | bytes 98312 | tf_op jit(solution)/shard_map/ppermute | solution.py:20
  86.1 6.9 %collective-permute-start.6 = (f32[32,2,6,1]{3,0,2,1:T(8,128)S(1)}, f32[32,2,6,1]{3,0,2,1:T(8,128)S(1)}, u32[]{:S(2)}, u32[]{:S(2)}) collective-permute-start(f32[32,2,6,1]{3,0,2,1:T(8,128)S(1)} %get-tuple-element.104), channel_id=1, source_target_pairs={{0,1},{1,2},{2,3},{3,4},{4,5},{5,6},{6,7},{8,9},{9,10},{10,11},{11... | collective-permute-start | bytes 4616 | tf_op jit(solution)/shard_map/ppermute | solution.py:19
  90.3 10.0 %collective-permute-start.7 = (f32[32,2,6,1]{3,0,2,1:T(8,128)S(1)}, f32[32,2,6,1]{3,0,2,1:T(8,128)S(1)}, u32[]{:S(2)}, u32[]{:S(2)}) collective-permute-start(f32[32,2,6,1]{3,0,2,1:T(8,128)S(1)} %get-tuple-element.103), channel_id=1, source_target_pairs={{1,0},{2,1},{3,2},{4,3},{5,4},{6,5},{7,6},{9,8},{10,9},{11,10},{12... | collective-permute-start | bytes 4616 | tf_op jit(solution)/shard_map/ppermute | solution.py:20
  114.1 10.5 %collective-permute-start.12 = (f32[32,2,1,128]{3,0,2,1:T(8,128)S(1)}, f32[32,2,1,128]{3,0,2,1:T(8,128)S(1)}, u32[]{:S(2)}, u32[]{:S(2)}) collective-permute-start(f32[32,2,1,128]{3,0,2,1:T(8,128)S(1)} %get-tuple-element.117), channel_id=1, source_target_pairs={{0,8},{8,16},{16,24},{24,32},{32,40},{40,48},{48,56},{56,64},{64,7... | collective-permute-start | bytes 98312 | tf_op jit(solution)/shard_map/ppermute | solution.py:19
  125.8 10.3 %collective-permute-start.14 = (f32[32,2,6,1]{3,0,2,1:T(8,128)S(1)}, f32[32,2,6,1]{3,0,2,1:T(8,128)S(1)}, u32[]{:S(2)}, u32[]{:S(2)}) collective-permute-start(f32[32,2,6,1]{3,0,2,1:T(8,128)S(1)} %get-tuple-element.95), channel_id=1, source_target_pairs={{0,1},{1,2},{2,3},{3,4},{4,5},{5,6},{6,7},{8,9},{9,10},{10,11},{11... | collective-permute-start | bytes 4616 | tf_op jit(solution)/shard_map/ppermute | solution.py:19
  133.0 10.7 %collective-permute-start.15 = (f32[32,2,6,1]{3,0,2,1:T(8,128)S(1)}, f32[32,2,6,1]{3,0,2,1:T(8,128)S(1)}, u32[]{:S(2)}, u32[]{:S(2)}) collective-permute-start(f32[32,2,6,1]{3,0,2,1:T(8,128)S(1)} %get-tuple-element.94), channel_id=1, source_target_pairs={{1,0},{2,1},{3,2},{4,3},{5,4},{6,5},{7,6},{9,8},{10,9},{11,10},{12... | collective-permute-start | bytes 4616 | tf_op jit(solution)/shard_map/ppermute | solution.py:20
  157.5 11.0 %collective-permute-start.20 = (f32[32,2,1,128]{3,0,2,1:T(8,128)S(1)}, f32[32,2,1,128]{3,0,2,1:T(8,128)S(1)}, u32[]{:S(2)}, u32[]{:S(2)}) collective-permute-start(f32[32,2,1,128]{3,0,2,1:T(8,128)S(1)} %get-tuple-element.110), channel_id=1, source_target_pairs={{0,8},{8,16},{16,24},{24,32},{32,40},{40,48},{48,56},{56,64},{64,7... | collective-permute-start | bytes 98312 | tf_op jit(solution)/shard_map/ppermute | solution.py:19
  163.4 5.2 %collective-permute-start.21 = (f32[32,2,1,128]{3,0,2,1:T(8,128)S(1)}, f32[32,2,1,128]{3,0,2,1:T(8,128)S(1)}, u32[]{:S(2)}, u32[]{:S(2)}) collective-permute-start(f32[32,2,1,128]{3,0,2,1:T(8,128)S(1)} %get-tuple-element.111), channel_id=1, source_target_pairs={{8,0},{16,8},{24,16},{32,24},{40,32},{48,40},{56,48},{64,56},{72,6... | collective-permute-start | bytes 98312 | tf_op jit(solution)/shard_map/ppermute | solution.py:20
  168.8 9.5 %collective-permute-start.22 = (f32[32,2,6,1]{3,0,2,1:T(8,128)S(1)}, f32[32,2,6,1]{3,0,2,1:T(8,128)S(1)}, u32[]{:S(2)}, u32[]{:S(2)}) collective-permute-start(f32[32,2,6,1]{3,0,2,1:T(8,128)S(1)} %get-tuple-element.86), channel_id=1, source_target_pairs={{0,1},{1,2},{2,3},{3,4},{4,5},{5,6},{6,7},{8,9},{9,10},{10,11},{11... | collective-permute-start | bytes 4616 | tf_op jit(solution)/shard_map/ppermute | solution.py:19
  175.3 7.4 %collective-permute-start.23 = (f32[32,2,6,1]{3,0,2,1:T(8,128)S(1)}, f32[32,2,6,1]{3,0,2,1:T(8,128)S(1)}, u32[]{:S(2)}, u32[]{:S(2)}) collective-permute-start(f32[32,2,6,1]{3,0,2,1:T(8,128)S(1)} %get-tuple-element.85), channel_id=1, source_target_pairs={{1,0},{2,1},{3,2},{4,3},{5,4},{6,5},{7,6},{9,8},{10,9},{11,10},{12... | collective-permute-start | bytes 4616 | tf_op jit(solution)/shard_map/ppermute | solution.py:20
  (13 other events, 46.0 us)
Sparse Core Ops, SparseCore 0:
  168.6 271.4 all-reduce.8
where the time goes:
time: 454 us; the launch traced here: 450 us
  waiting for transfers between devices  271 us (60%)
  starting transfers between devices  79.2 us (17%)
  matrix products  71 us (16%)
  between operations  17 us (4%)
  local copies, waits for them, and re-layouts  6.29 us (1%)
  other arithmetic  5.92 us (1%)
    psum x1, waiting for transfers between devices, per_device(): results.append(lax.psum(terms, ('gx', 'gy')) * factor)  248 us
    ppermute x12, starting transfers between devices, with_halo(): before = lax.ppermute(last, axis, up)  58.7 us
    dot_general x81, matrix products, back_taps(): jnp.einsum('oi,ozxy->izxy', kernel[tap], window, precision=lax.Precision....  27.5 us
    dot_general x81, matrix products, conv_taps(): jnp.einsum('oi,izxy->ozxy', kernel[tap], window, precision=lax.Precision....  23.8 us
    ppermute x12, waiting for transfers between devices, with_halo(): after = lax.ppermute(leading, axis, down)  20.7 us
    ppermute x12, starting transfers between devices, with_halo(): after = lax.ppermute(leading, axis, down)  20.4 us
    dot_general x81, matrix products, kernel_terms(): jnp.einsum('ozxy,izxy->oi', slope_grad, window, precision=lax.Precision.H...  19.7 us
  transfers between devices with their start and end apart: 25, of which 9 were waited for; matrix products, arithmetic and copies ran while one was open for 8% of the time, Pallas kernels for 0%

commit v1 on v0

v1 whole, which is shorter than its diff:
```python
import functools
import math

import jax
import jax.numpy as jnp
from jax import lax
from jax.experimental import pallas as pl
from jax.experimental.pallas import tpu as pltpu
from jax.sharding import PartitionSpec as P

MESH = pl.DeviceIdType.MESH
F32, BF16 = jnp.float32, jnp.bfloat16
INV_ROOT_TWO = 0.7071067811865476
INV_ROOT_TWO_PI = 0.3989422804014327
SIDES = ((-1, -1), (0, -1), (1, -1), (-1, 1), (0, 1), (1, 1))


def gelu_slope(value):
    normal_cdf = 0.5 * (1.0 + lax.erf(value * INV_ROOT_TWO))
    density = jnp.exp(-0.5 * value * value) * INV_ROOT_TWO_PI
    return normal_cdf + value * density


def split(value):
    high = value.astype(BF16)
    low = (value - high.astype(F32)).astype(BF16)
    return high, low


def roll(value, shift):
    shift = shift % 128
    return value if shift == 0 else pltpu.roll(value, shift, 1)


def lanes(rows):
    return lax.broadcasted_iota(jnp.int32, (rows, 128), 1)


def step_kernel(
    dims, x3_in, cot_in, x2_in, x1_in, k3_in, k2_in, k1_in,
    gin_ref, red_ref,
    x3, cot, x2, x1, k3, k2, k1,
    send, recv, field, weights, hmat, prod, slope,
    part, rs_recv, z_recv, ag_recv,
    load_sem, halo_send, halo_recv, rs_send_sem, rs_recv_sem, z_send_sem, z_recv_sem, ag_send_sem, ag_recv_sem,
):
    gxn, gyn, zn, ylo = dims
    members = ylo * 2 * gyn
    per = 32 // members
    gx, gy = lax.axis_index("gx"), lax.axis_index("gy")
    core, my_z, my_y = gx % 2, gx // 2 % zn, gx // (2 * zn)
    me = (my_y * 2 + core) * gyn + gy

    def member(m):
        row = m // gyn
        return (row // 2 * (2 * zn) + my_z * 2 + row % 2, m % gyn)

    def z_peer(k):
        return (my_y * (2 * zn) + k * 2 + core, gy)

    def near(n, side):
        return ((gx + n + gxn) % gxn, (gy + side + gyn) % gyn)

    loads = []
    for i, (src, dst) in enumerate(
        ((x3_in, x3), (k3_in, k3), (cot_in, cot), (x2_in, x2), (x1_in, x1), (k2_in, k2), (k1_in, k1))
    ):
        copy = pltpu.make_async_copy(src, dst, load_sem.at[i])
        copy.start()
        loads.append(copy)

    barrier = pltpu.get_barrier_semaphore()
    around = [near(n, s) for n, s in SIDES] + [near(-1, 0), near(1, 0)]
    for device in around:
        pl.semaphore_signal(barrier, inc=1, device_id=device, device_id_type=MESH)

    def greet_member(k, carry):
        pl.semaphore_signal(barrier, inc=1, device_id=member((me + k) % members), device_id_type=MESH)
        return carry

    def greet_z(k, carry):
        pl.semaphore_signal(barrier, inc=1, device_id=z_peer((my_z + k) % zn), device_id_type=MESH)
        return carry

    lax.fori_loop(1, members, greet_member, 0)
    lax.fori_loop(1, zn, greet_z, 0)

    up = (gx > 0).astype(F32)
    down = (gx < gxn - 1).astype(F32)
    left = (gy > 0).astype(F32)
    right = (gy < gyn - 1).astype(F32)
    lane8, lane32 = lanes(8), lanes(32)
    zero32 = jnp.zeros((32, 128), F32)

    for bi in range(4):
        for part_row in (0, 256):
            for z in range(2):
                base = part_row + z * 128 + 96
                field[bi, base : base + 32, :] = jnp.zeros((32, 640), BF16)

    def load_tiles(ref):
        return [[ref[pl.ds(z * 4 + x, 32, stride=8), :] for x in range(4)] for z in range(2)]

    def edge_columns(tiles):
        packed = []
        for z in range(2):
            total = zero32
            for x in range(4):
                keep = (lane32 == 8 * x) | (lane32 == (8 * x - 1) % 128)
                total = jnp.where(keep, roll(tiles[z][x], 8 * x), total)
            packed.append(total)
        return packed

    def fill_send(f, tiles, packed):
        for z in range(2):
            send[f, z * 32 : z * 32 + 32, :] = tiles[z][0]
            send[f, 64 + z * 32 : 96 + z * 32, :] = tiles[z][3]
        squeezed = None
        for z in range(2):
            for v in range(4):
                term = roll(packed[z][8 * v : 8 * v + 8], 2 * v + 64 * z)
                squeezed = term if squeezed is None else squeezed + term
        send[f, 128:136, :] = squeezed

    def fill_own(bi, tiles):
        for z in range(2):
            for x_in in range(4):
                high, low = split(tiles[z][x_in])
                for b in range(3):
                    x = x_in + 1 - b
                    if 0 <= x < 4:
                        row, col = z * 128 + b * 32, x * 128
                        field[bi, row : row + 32, col : col + 128] = high
                        field[bi, 256 + row : 288 + row, col : col + 128] = low

    def halo_copies(f):
        copies = []

        def add(lo, hi, at, device):
            copies.append(
                pltpu.make_async_remote_copy(
                    src_ref=send.at[f, pl.ds(lo, hi - lo)],
                    dst_ref=recv.at[f, pl.ds(at, hi - lo)],
                    send_sem=halo_send.at[f],
                    recv_sem=halo_recv.at[f],
                    device_id=device,
                    device_id_type=MESH,
                )
            )

        for k, (n, s) in enumerate(SIDES):
            add(128, 136, 128 + 8 * k, near(-n, -s))
        add(64, 128, 0, near(1, 0))
        add(0, 64, 64, near(-1, 0))
        return copies

    def start_halo(f):
        for copy in halo_copies(f):
            copy.start()

    def whole_halo(f):
        return pltpu.make_async_remote_copy(
            src_ref=recv.at[f], dst_ref=recv.at[f], send_sem=halo_send.at[f], recv_sem=halo_recv.at[f],
            device_id=near(1, 0), device_id_type=MESH,
        )

    def fill_halo(bi, f):
        for z in range(2):
            for at, b, x, ok in ((0, 0, 0, up), (64, 2, 3, down)):
                high, low = split(recv[f, at + z * 32 : at + z * 32 + 32, :] * ok)
                row, col = z * 128 + b * 32, x * 128
                field[bi, row : row + 32, col : col + 128] = high
                field[bi, 256 + row : 288 + row, col : col + 128] = low
        first = ((lane8 & 63) >= 55) & ((lane8 & 63) <= 62)
        last = ((lane8 & 63) >= 31) & ((lane8 & 63) <= 38)
        merged = []
        for k, ok in ((0, left), (3, right)):
            tile = [recv[f, 128 + 8 * (k + j) : 136 + 8 * (k + j), :] for j in range(3)]
            total = tile[1]
            total = total + jnp.where(first, roll(tile[0], 96), 0.0) * up
            total = total + jnp.where(last, roll(tile[2], 32), 0.0) * down
            merged.append(total * ok)
        both = jnp.where(lane8 % 2 == 1, roll(merged[0], 2), merged[1])
        for z in range(2):
            for b in range(3):
                tile = jnp.concatenate([roll(both, 7 - 2 * v - 64 * z - 8 * b) for v in range(4)], axis=0)
                high, low = split(tile)
                row = z * 128 + b * 32
                field[bi, row : row + 32, 512:640] = high
                field[bi, 256 + row : 288 + row, 512:640] = low

    def row_block(kernel, a, c):
        return jnp.concatenate(
            [kernel[9 * a + 3 * b + c] for b in range(3)] + [jnp.zeros((32, 32), F32)], axis=1
        )

    def store_weights(wi, row, col, tile):
        high, low = split(tile)
        weights[wi, row : row + 32, col : col + 128] = high
        weights[wi, row : row + 32, 256 + col : 384 + col] = high
        weights[wi, row : row + 32, 512 + col : 640 + col] = low

    def build_weights(layer, kernel):
        for a in range(3):
            blocks = [row_block(kernel, a, c) for c in range(3)]
            flipped = jnp.concatenate(blocks + [zero32], axis=0).T
            for c in range(3):
                back = jnp.concatenate(
                    [
                        flipped[(2 - b) * 32 : (3 - b) * 32, (2 - c) * 32 : (3 - c) * 32]
                        for b in range(3)
                    ]
                    + [jnp.zeros((32, 32), F32)],
                    axis=1,
                )
                for z in range(2):
                    zp = a + z - 1
                    if 0 <= zp < 2:
                        store_weights(layer, c * 64 + z * 32, zp * 128, blocks[c])
                        store_weights(3 + layer, c * 64 + zp * 32, z * 128, back)

    def conv(wi, bi):
        for lo, hi in ((0, 256), (256, 512), (512, 640)):
            prod[:, lo:hi] = jnp.dot(
                weights[wi, :, 0:512], field[bi, :, lo:hi], preferred_element_type=F32
            ) + jnp.dot(weights[wi, :, 512:768], field[bi, 0:256, lo:hi], preferred_element_type=F32)
        out = []
        for z in range(2):
            row = z * 32
            edge = jnp.where(
                lane32 % 8 == 0, prod[row : row + 32, 512:640], prod[128 + row : 160 + row, 512:640]
            )
            tiles = []
            for x in range(4):
                col = x * 128
                at_edge = roll(edge, -8 * x)
                before = roll(prod[row : row + 32, col : col + 128], 1)
                after = roll(prod[128 + row : 160 + row, col : col + 128], -1)
                tiles.append(
                    prod[64 + row : 96 + row, col : col + 128]
                    + jnp.where(lane32 == 0, at_edge, before)
                    + jnp.where(lane32 == 127, at_edge, after)
                )
            out.append(tiles)
        return out

    def store_h(c, z, col, tile):
        high, low = split(tile)
        row = c * 64 + z * 32
        hmat[row : row + 32, col : col + 128] = high
        hmat[192 + row : 224 + row, col : col + 128] = low

    def kernel_grad(layer, bi, tiles, packed):
        for z in range(2):
            for x in range(4):
                col = x * 128
                store_h(0, z, col, jnp.where(lane32 == 127, 0.0, roll(tiles[z][x], -1)))
                store_h(1, z, col, tiles[z][x])
                store_h(2, z, col, jnp.where(lane32 == 0, 0.0, roll(tiles[z][x], 1)))
            store_h(0, z, 512, jnp.where(lane32 % 8 == 0, packed[z], 0.0))
            store_h(1, z, 512, zero32)
            store_h(2, z, 512, jnp.where(lane32 % 8 == 7, packed[z], 0.0))
        contract = (((1,), (1,)), ((), ()))
        main = lax.dot_general(hmat[...], field[bi, 0:256, :], contract, preferred_element_type=F32)
        rest = lax.dot_general(hmat[0:192, :], field[bi, 256:512, :], contract, preferred_element_type=F32)
        total = main[0:192] + main[192:384] + rest
        blocks = []
        for c in range(3):
            top, low = total[c * 64 : c * 64 + 32], total[c * 64 + 32 : c * 64 + 64]
            blocks += [low[:, 0:128], top[:, 0:128] + low[:, 128:256], top[:, 128:256]]
        for j in range(8):
            block = blocks[j]
            if j < 3:
                block = jnp.where(lane32 >= 96, roll(blocks[8], 96 - 32 * j), block)
            part[layer, 4 * j : 4 * j + 4] = block.reshape(4, 8, 128)

    def group_copy(src, dst, send_sem, recv_sem, device):
        return pltpu.make_async_remote_copy(
            src_ref=src, dst_ref=dst, send_sem=send_sem, recv_sem=recv_sem, device_id=device, device_id_type=MESH
        )

    def rs_start(layer):
        def body(k, carry):
            m = (me + k) % members
            group_copy(
                part.at[layer, pl.ds(m * per, per)], rs_recv.at[layer, pl.ds(me * per, per)],
                rs_send_sem.at[layer], rs_recv_sem.at[layer], member(m),
            ).start()
            return carry

        lax.fori_loop(1, members, body, 0)
        rs_recv[layer, pl.ds(me * per, per)] = part[layer, pl.ds(me * per, per)]

    def rs_wait(layer):
        count = (members - 1) * per
        return group_copy(
            part.at[layer, pl.ds(0, count)], rs_recv.at[layer, pl.ds(0, count)],
            rs_send_sem.at[layer], rs_recv_sem.at[layer], near(1, 0),
        )

    def z_start(layer):
        rs_wait(layer).wait_recv()
        total = rs_recv[layer, 0:per]
        for m in range(1, members):
            total = total + rs_recv[layer, m * per : m * per + per]
        z_recv[layer, my_z] = total

        def body(k, carry):
            group_copy(
                z_recv.at[layer, my_z], z_recv.at[layer, my_z],
                z_send_sem.at[layer], z_recv_sem.at[layer], z_peer((my_z + k) % zn),
            ).start()
            return carry

        lax.fori_loop(1, zn, body, 0)

    def z_wait(layer):
        return group_copy(
            z_recv.at[layer, pl.ds(0, zn - 1)], z_recv.at[layer, pl.ds(0, zn - 1)],
            z_send_sem.at[layer], z_recv_sem.at[layer], near(1, 0),
        )

    def ag_start(layer):
        z_wait(layer).wait_recv()
        total = z_recv[layer, 0]
        for k in range(1, zn):
            total = total + z_recv[layer, k]
        mine = pl.ds(me * per, per)
        ag_recv[layer, mine] = total

        def body(k, carry):
            group_copy(
                ag_recv.at[layer, mine], ag_recv.at[layer, mine],
                ag_send_sem.at[layer], ag_recv_sem.at[layer], member((me + k) % members),
            ).start()
            return carry

        lax.fori_loop(1, members, body, 0)

    def ag_wait(layer):
        count = pl.ds(0, (members - 1) * per)
        return group_copy(
            ag_recv.at[layer, count], ag_recv.at[layer, count],
            ag_send_sem.at[layer], ag_recv_sem.at[layer], near(1, 0),
        )

    def finish(layer):
        ag_wait(layer).wait_recv()
        red_ref[layer] = ag_recv[layer]

    loads[0].wait()
    tiles = load_tiles(x3)
    fill_send(0, tiles, edge_columns(tiles))
    pl.semaphore_wait(barrier, len(around) + members - 1 + zn - 1)
    start_halo(0)
    fill_own(0, tiles)
    for f, ref, at in ((1, x2, 3), (2, x1, 4)):
        loads[at].wait()
        tiles = load_tiles(ref)
        fill_send(f, tiles, edge_columns(tiles))
        start_halo(f)
        fill_own(f, tiles)
    loads[1].wait()
    build_weights(0, k3)
    loads[2].wait()
    loads[5].wait()
    loads[6].wait()
    grad = load_tiles(cot)

    for layer in range(3):
        if layer == 0:
            whole_halo(0).wait_recv()
            fill_halo(0, 0)
            pre = conv(0, 0)
            mult = [[gelu_slope(pre[z][x]) for x in range(4)] for z in range(2)]
        else:
            mult = [
                [slope[layer - 1, (z * 4 + x) * 32 : (z * 4 + x) * 32 + 32, :] for x in range(4)] for z in range(2)
            ]
        h = [[grad[z][x] * mult[z][x] for x in range(4)] for z in range(2)]
        packed = edge_columns(h)
        fill_send(3 + layer, h, packed)
        start_halo(3 + layer)
        fill_own(3, h)
        kernel_grad(layer, layer, h, packed)
        rs_start(layer)
        if layer < 2:
            build_weights(layer + 1, (k2, k1)[layer])
            whole_halo(layer + 1).wait_recv()
            fill_halo(layer + 1, layer + 1)
            pre = conv(layer + 1, layer + 1)
            for z in range(2):
                for x in range(4):
                    at = (z * 4 + x) * 32
                    slope[layer, at : at + 32, :] = gelu_slope(pre[z][x])
        whole_halo(3 + layer).wait_recv()
        fill_halo(3, 3 + layer)
        grad = conv(3 + layer, 3)
        if layer == 1:
            z_start(0)
    for z in range(2):
        for x in range(4):
            gin_ref[pl.ds(z * 4 + x, 32, stride=8), :] = grad[z][x]
    z_start(1)
    ag_start(0)
    z_start(2)
    ag_start(1)
    finish(0)
    ag_start(2)
    finish(1)
    finish(2)
    for f in range(6):
        whole_halo(f).wait_send()
    for layer in range(3):
        rs_wait(layer).wait_send()
        z_wait(layer).wait_send()
        ag_wait(layer).wait_send()


def unpack_kernel(factor, gin_in, red_ref, gin_ref, out3, out2, out1):
    gin_ref[...] = gin_in[...]
    for layer, out in enumerate((out3, out2, out1)):
        for a in range(3):
            for b in range(3):
                for c in range(3):
                    j = c * 3 + a
                    row, col = (j * 32, b * 32) if j < 8 else (b * 32, 96)
                    out[9 * a + 3 * b + c] = red_ref[layer, row : row + 32, col : col + 32] * factor


def per_device(dims, factor, x1, x2, x3, cot, k1, k2, k3):
    flat = [v.reshape(256, 128) for v in (x3, cot, x2, x1)]
    vmem = pl.BlockSpec(memory_space=pltpu.VMEM)
    anywhere = pl.BlockSpec(memory_space=pl.ANY)
    members = dims[3] * 2 * dims[1]
    per = 32 // members
    dma = pltpu.SemaphoreType.DMA
    gin, red = pl.pallas_call(
        functools.partial(step_kernel, dims),
        out_shape=(jax.ShapeDtypeStruct((256, 128), F32), jax.ShapeDtypeStruct((3, 32, 8, 128), F32)),
        in_specs=[anywhere] * 7,
        out_specs=(vmem, vmem),
        scratch_shapes=[pltpu.VMEM((256, 128), F32)] * 4
        + [pltpu.VMEM((27, 32, 32), F32)] * 3
        + [
            pltpu.VMEM((6, 136, 128), F32),
            pltpu.VMEM((6, 176, 128), F32),
            pltpu.VMEM((4, 512, 640), BF16),
            pltpu.VMEM((6, 192, 768), BF16),
            pltpu.VMEM((384, 640), BF16),
            pltpu.VMEM((192, 640), F32),
            pltpu.VMEM((2, 256, 128), F32),
            pltpu.VMEM((3, 32, 8, 128), F32),
            pltpu.VMEM((3, 32, 8, 128), F32),
            pltpu.VMEM((3, dims[2], per, 8, 128), F32),
            pltpu.VMEM((3, 32, 8, 128), F32),
            dma((7,)), dma((6,)), dma((6,)), dma((3,)), dma((3,)), dma((3,)), dma((3,)), dma((3,)), dma((3,)),
        ],
        compiler_params=pltpu.CompilerParams(
            collective_id=0, has_side_effects=True, vmem_limit_bytes=67043328
        ),
        name="step",
    )(*flat, k3, k2, k1)
    shape = jax.ShapeDtypeStruct(k1.shape, F32)
    gin, out3, out2, out1 = pl.pallas_call(
        functools.partial(unpack_kernel, factor),
        out_shape=(jax.ShapeDtypeStruct((256, 128), F32), shape, shape, shape),
        in_specs=[vmem] * 2,
        out_specs=(vmem,) * 4,
        name="unpack",
    )(gin, red.reshape(3, 256, 128))
    return gin.reshape(x1.shape), out1, out2, out3


def solution(mesh):
    gxn, gyn = mesh.shape["gx"], mesh.shape["gy"]
    zn = min(8, gxn // 2)
    dims = (gxn, gyn, zn, gxn // (2 * zn))
    factor = 1.0 / math.sqrt(2 * 4 * 128 * gxn * gyn)
    placed = P(None, None, "gx", "gy")
    return jax.shard_map(
        functools.partial(per_device, dims, factor),
        mesh=mesh,
        in_specs=(placed,) * 4 + (P(),) * 3,
        out_specs=(placed, P(), P(), P()),
        check_vma=False,
    )
```

time: 454 us -> 49.8 us (0.11)
  waiting for transfers between devices: 271 us -> 0 us
  starting transfers between devices: 79.2 us -> 0 us
  matrix products: 71 us -> 0 us
  Pallas kernels: 0 us -> 49 us
  between operations: 17 us -> 0.64 us
  local copies, waits for them, and re-layouts: 6.29 us -> 0 us
  other arithmetic: 5.92 us -> 0 us
    psum x1 -> x0, waiting for transfers between devices: 248 us -> none  [per_device(): results.append(lax.psum(terms, ('gx', 'gy')) * factor)]
    ppermute x24 -> x0, starting transfers between devices: 79.1 us -> none  [the longest x12 58.7 us: with_halo(): before = lax.ppermute(last, axis, up)]
    dot_general x243 -> x0, matrix products: 71 us -> none  [the longest x81 27.5 us: back_taps(): jnp.einsum('oi,ozxy->izxy', kernel[tap], window, precision=lax.Precision....]
    pallas_call x0 -> x2, Pallas kernels: none -> 49 us  [the longest x1 46.6 us: per_device(): pl.pallas_call(functools.partial(step_kernel, dims), out_shape=(jax.Shape...]
    ppermute x24 -> x0, waiting for transfers between devices: 22.8 us -> none  [the longest x12 20.7 us: with_halo(): after = lax.ppermute(leading, axis, down)]
  transfers between devices with their start and end apart: 25 -> 0, of which waited for: 9 -> 0; matrix products, arithmetic and copies ran while one was open for 8% -> 0% of each run, Pallas kernels for 0% -> 0%
where the time goes in v1:
time: 49.8 us; the launch traced here: 49.7 us
  Pallas kernels  49 us (98%)
  between operations  0.64 us (1%)
    pallas_call x1, Pallas kernels, per_device(): pl.pallas_call(functools.partial(step_kernel, dims), out_shape=(jax.Shape...  46.6 us
    pallas_call x1, Pallas kernels, per_device(): pl.pallas_call(functools.partial(unpack_kernel, factor), out_shape=(jax.S...  2.41 us

profile of v1, /device:TPU:1, one launch (start us, length us, event | category | flops | bytes accessed | tf_op | source)
XLA Modules:
  0.0 49.7 jit_solution(16166343740424066798)
XLA Ops:
  0.6 46.6 %step.1 = (f32[256,128]{1,0:T(8,128)}, f32[3,32,8,128]{3,2,1,0:T(8,128)}) custom-call(f32[256,128]{1,0:T(8,128)} %bitcast.7, f32[256,128]{1,0:T(8,128)} %bitcast.8, f32[256,128]{1,0:T(8,128)} %bitcast.9, f32[256,128]{1,0:T(8,128)} %bitcast.10, f32[27,32,32]{2,1,0:T(8,128)} %k3_in.1, f32[27,32,32]{2,1,0:T(8,128)} %k2_in.1, f32[27,32,32]{2,1,0:T(8,128)} %k1_in.1), custom_call_target="tpu_custom_call" | custom-call | tf_op jit(solution)/shard_map/step/pallas_call | solution.py:438
  47.2 2.4 %unpack.1 = (f32[256,128]{1,0:T(8,128)}, f32[27,32,32]{2,1,0:T(8,128)}, f32[27,32,32]{2,1,0:T(8,128)}, f32[27,32,32]{2,1,0:T(8,128)}) custom-call(f32[256,128]{1,0:T(8,128)} %get-tuple-element.10.gin_in, f32[3,256,128]{2,1,0:T(8,128)} %bitcast.6), custom_call_target="tpu_custom_call" | custom-call | tf_op jit(solution)/shard_map/unpack/pallas_call | solution.py:465

commit v2 on v1

--- a/solution.py
+++ b/solution.py
@@ -48,18 +48,20 @@
     members = ylo * 2 * gyn
     per = 32 // members
     gx, gy = lax.axis_index("gx"), lax.axis_index("gy")
-    core, my_z, my_y = gx % 2, gx // 2 % zn, gx // (2 * zn)
+    core, my_z, my_y = lax.rem(gx, 2), lax.rem(lax.div(gx, 2), zn), lax.div(gx, 2 * zn)
     me = (my_y * 2 + core) * gyn + gy
 
-    def member(m):
-        row = m // gyn
-        return (row // 2 * (2 * zn) + my_z * 2 + row % 2, m % gyn)
-
-    def z_peer(k):
-        return (my_y * (2 * zn) + k * 2 + core, gy)
+    lines = []
+    for ky in range(ylo):
+        for kc in range(2):
+            other_y, other_core = lax.rem(my_y + ky, ylo), lax.rem(core + kc, 2)
+            lines.append((other_y * (2 * zn) + my_z * 2 + other_core, (other_y * 2 + other_core) * gyn))
+    spots = [lax.rem(gy + k, gyn) for k in range(gyn)]
+    peers = [((at, spot), base + spot) for spot in spots for at, base in lines][1:]
+    z_peers = [(my_y * (2 * zn) + lax.rem(my_z + k, zn) * 2 + core, gy) for k in range(1, zn)]
 
     def near(n, side):
-        return ((gx + n + gxn) % gxn, (gy + side + gyn) % gyn)
+        return (lax.rem(gx + n + gxn, gxn), lax.rem(gy + side + gyn, gyn))
 
     loads = []
     for i, (src, dst) in enumerate(
@@ -71,19 +73,9 @@
 
     barrier = pltpu.get_barrier_semaphore()
     around = [near(n, s) for n, s in SIDES] + [near(-1, 0), near(1, 0)]
-    for device in around:
+    greeted = around + [device for device, _ in peers] + z_peers
+    for device in greeted:
         pl.semaphore_signal(barrier, inc=1, device_id=device, device_id_type=MESH)
-
-    def greet_member(k, carry):
-        pl.semaphore_signal(barrier, inc=1, device_id=member((me + k) % members), device_id_type=MESH)
-        return carry
-
-    def greet_z(k, carry):
-        pl.semaphore_signal(barrier, inc=1, device_id=z_peer((my_z + k) % zn), device_id_type=MESH)
-        return carry
-
-    lax.fori_loop(1, members, greet_member, 0)
-    lax.fori_loop(1, zn, greet_z, 0)
 
     up = (gx > 0).astype(F32)
     down = (gx < gxn - 1).astype(F32)
@@ -163,6 +155,9 @@
             src_ref=recv.at[f], dst_ref=recv.at[f], send_sem=halo_send.at[f], recv_sem=halo_recv.at[f],
             device_id=near(1, 0), device_id_type=MESH,
         )
+
+    def halo_wait(f):
+        whole_halo(f).wait_recv()
 
     def fill_halo(bi, f):
         for z in range(2):
@@ -280,15 +275,11 @@
         )
 
     def rs_start(layer):
-        def body(k, carry):
-            m = (me + k) % members
+        for device, m in peers:
             group_copy(
                 part.at[layer, pl.ds(m * per, per)], rs_recv.at[layer, pl.ds(me * per, per)],
-                rs_send_sem.at[layer], rs_recv_sem.at[layer], member(m),
+                rs_send_sem.at[layer], rs_recv_sem.at[layer], device,
             ).start()
-            return carry
-
-        lax.fori_loop(1, members, body, 0)
         rs_recv[layer, pl.ds(me * per, per)] = part[layer, pl.ds(me * per, per)]
 
     def rs_wait(layer):
@@ -305,14 +296,10 @@
             total = total + rs_recv[layer, m * per : m * per + per]
         z_recv[layer, my_z] = total
 
-        def body(k, carry):
+        for device in z_peers:
             group_copy(
-                z_recv.at[layer, my_z], z_recv.at[layer, my_z],
-                z_send_sem.at[layer], z_recv_sem.at[layer], z_peer((my_z + k) % zn),
+                z_recv.at[layer, my_z], z_recv.at[layer, my_z], z_send_sem.at[layer], z_recv_sem.at[layer], device
             ).start()
-            return carry
-
-        lax.fori_loop(1, zn, body, 0)
 
     def z_wait(layer):
         return group_copy(
@@ -328,14 +315,10 @@
         mine = pl.ds(me * per, per)
         ag_recv[layer, mine] = total
 
-        def body(k, carry):
+        for device, _ in peers:
             group_copy(
-                ag_recv.at[layer, mine], ag_recv.at[layer, mine],
-                ag_send_sem.at[layer], ag_recv_sem.at[layer], member((me + k) % members),
+                ag_recv.at[layer, mine], ag_recv.at[layer, mine], ag_send_sem.at[layer], ag_recv_sem.at[layer], device
             ).start()
-            return carry
-
-        lax.fori_loop(1, members, body, 0)
 
     def ag_wait(layer):
         count = pl.ds(0, (members - 1) * per)
@@ -348,97 +331,106 @@
         ag_wait(layer).wait_recv()
         red_ref[layer] = ag_recv[layer]
 
-    loads[0].wait()
-    tiles = load_tiles(x3)
-    fill_send(0, tiles, edge_columns(tiles))
-    pl.semaphore_wait(barrier, len(around) + members - 1 + zn - 1)
-    start_halo(0)
-    fill_own(0, tiles)
-    for f, ref, at in ((1, x2, 3), (2, x1, 4)):
-        loads[at].wait()
-        tiles = load_tiles(ref)
-        fill_send(f, tiles, edge_columns(tiles))
-        start_halo(f)
-        fill_own(f, tiles)
-    loads[1].wait()
-    build_weights(0, k3)
-    loads[2].wait()
-    loads[5].wait()
-    loads[6].wait()
-    grad = load_tiles(cot)
-
+    def sequence():
+        loads[0].wait()
+        tiles = load_tiles(x3)
+        fill_send(0, tiles, edge_columns(tiles))
+        pl.semaphore_wait(barrier, len(greeted))
+        start_halo(0)
+        fill_own(0, tiles)
+        for f, ref, at in ((1, x2, 3), (2, x1, 4)):
+            loads[at].wait()
+            tiles = load_tiles(ref)
+            fill_send(f, tiles, edge_columns(tiles))
+            start_halo(f)
+            fill_own(f, tiles)
+        loads[1].wait()
+        build_weights(0, k3)
+        loads[2].wait()
+        loads[5].wait()
+        loads[6].wait()
+        grad = load_tiles(cot)
+
+        for layer in range(3):
+            if layer == 0:
+                halo_wait(0)
+                fill_halo(0, 0)
+                pre = conv(0, 0)
+                mult = [[gelu_slope(pre[z][x]) for x in range(4)] for z in range(2)]
+            else:
+                mult = [
+                    [slope[layer - 1, (z * 4 + x) * 32 : (z * 4 + x) * 32 + 32, :] for x in range(4)] for z in range(2)
+                ]
+            h = [[grad[z][x] * mult[z][x] for x in range(4)] for z in range(2)]
+            packed = edge_columns(h)
+            fill_send(3 + layer, h, packed)
+            start_halo(3 + layer)
+            fill_own(3, h)
+            kernel_grad(layer, layer, h, packed)
+            rs_start(layer)
+            if layer < 2:
+                build_weights(layer + 1, (k2, k1)[layer])
+                halo_wait(layer + 1)
+                fill_halo(layer + 1, layer + 1)
+                pre = conv(layer + 1, layer + 1)
+                for z in range(2):
+                    for x in range(4):
+                        at = (z * 4 + x) * 32
+                        slope[layer, at : at + 32, :] = gelu_slope(pre[z][x])
+            halo_wait(3 + layer)
+            fill_halo(3, 3 + layer)
+            grad = conv(3 + layer, 3)
+            if layer == 1:
+                z_start(0)
+        for z in range(2):
+            for x in range(4):
+                gin_ref[pl.ds(z * 4 + x, 32, stride=8), :] = grad[z][x]
+        z_start(1)
+        ag_start(0)
+        z_start(2)
+        ag_start(1)
+        finish(0)
+        ag_start(2)
+        finish(1)
+        finish(2)
+        for f in range(6):
+            whole_halo(f).wait_send()
+        for layer in range(3):
+            rs_wait(layer).wait_send()
+            z_wait(layer).wait_send()
+            ag_wait(layer).wait_send()
+
+    sequence()
+
+
+def unpack_kernel(factor, gin_in, red_ref, gin_out, *refs):
+    outs, held, sem = refs[0:3], refs[3:6], refs[6]
+    copies = [pltpu.make_async_copy(gin_in, gin_out, sem.at[3])]
+    copies[0].start()
     for layer in range(3):
-        if layer == 0:
-            whole_halo(0).wait_recv()
-            fill_halo(0, 0)
-            pre = conv(0, 0)
-            mult = [[gelu_slope(pre[z][x]) for x in range(4)] for z in range(2)]
-        else:
-            mult = [
-                [slope[layer - 1, (z * 4 + x) * 32 : (z * 4 + x) * 32 + 32, :] for x in range(4)] for z in range(2)
-            ]
-        h = [[grad[z][x] * mult[z][x] for x in range(4)] for z in range(2)]
-        packed = edge_columns(h)
-        fill_send(3 + layer, h, packed)
-        start_halo(3 + layer)
-        fill_own(3, h)
-        kernel_grad(layer, layer, h, packed)
-        rs_start(layer)
-        if layer < 2:
-            build_weights(layer + 1, (k2, k1)[layer])
-            whole_halo(layer + 1).wait_recv()
-            fill_halo(layer + 1, layer + 1)
-            pre = conv(layer + 1, layer + 1)
-            for z in range(2):
-                for x in range(4):
-                    at = (z * 4 + x) * 32
-                    slope[layer, at : at + 32, :] = gelu_slope(pre[z][x])
-        whole_halo(3 + layer).wait_recv()
-        fill_halo(3, 3 + layer)
-        grad = conv(3 + layer, 3)
-        if layer == 1:
-            z_start(0)
-    for z in range(2):
-        for x in range(4):
-            gin_ref[pl.ds(z * 4 + x, 32, stride=8), :] = grad[z][x]
-    z_start(1)
-    ag_start(0)
-    z_start(2)
-    ag_start(1)
-    finish(0)
-    ag_start(2)
-    finish(1)
-    finish(2)
-    for f in range(6):
-        whole_halo(f).wait_send()
-    for layer in range(3):
-        rs_wait(layer).wait_send()
-        z_wait(layer).wait_send()
-        ag_wait(layer).wait_send()
-
-
-def unpack_kernel(factor, gin_in, red_ref, gin_ref, out3, out2, out1):
-    gin_ref[...] = gin_in[...]
-    for layer, out in enumerate((out3, out2, out1)):
         for a in range(3):
             for b in range(3):
                 for c in range(3):
                     j = c * 3 + a
                     row, col = (j * 32, b * 32) if j < 8 else (b * 32, 96)
-                    out[9 * a + 3 * b + c] = red_ref[layer, row : row + 32, col : col + 32] * factor
+                    held[layer][9 * a + 3 * b + c] = red_ref[layer, row : row + 32, col : col + 32] * factor
+        copies.append(pltpu.make_async_copy(held[layer], outs[layer], sem.at[layer]))
+        copies[-1].start()
+    for copy in copies:
+        copy.wait()
 
 
 def per_device(dims, factor, x1, x2, x3, cot, k1, k2, k3):
     flat = [v.reshape(256, 128) for v in (x3, cot, x2, x1)]
     vmem = pl.BlockSpec(memory_space=pltpu.VMEM)
-    anywhere = pl.BlockSpec(memory_space=pl.ANY)
+    hbm = pl.BlockSpec(memory_space=pltpu.HBM)
     members = dims[3] * 2 * dims[1]
     per = 32 // members
     dma = pltpu.SemaphoreType.DMA
     gin, red = pl.pallas_call(
         functools.partial(step_kernel, dims),
         out_shape=(jax.ShapeDtypeStruct((256, 128), F32), jax.ShapeDtypeStruct((3, 32, 8, 128), F32)),
-        in_specs=[anywhere] * 7,
+        in_specs=[hbm] * 7,
         out_specs=(vmem, vmem),
         scratch_shapes=[pltpu.VMEM((256, 128), F32)] * 4
         + [pltpu.VMEM((27, 32, 32), F32)] * 3
@@ -457,16 +449,18 @@
             dma((7,)), dma((6,)), dma((6,)), dma((3,)), dma((3,)), dma((3,)), dma((3,)), dma((3,)), dma((3,)),
         ],
         compiler_params=pltpu.CompilerParams(
-            collective_id=0, has_side_effects=True, vmem_limit_bytes=67043328
+            collective_id=0, has_side_effects=True, vmem_limit_bytes=40 * 1024 * 1024
         ),
         name="step",
-    )(*flat, k3, k2, k1)
+    )(*[pltpu.with_memory_space_constraint(v, pltpu.HBM) for v in (*flat, k3, k2, k1)])
     shape = jax.ShapeDtypeStruct(k1.shape, F32)
     gin, out3, out2, out1 = pl.pallas_call(
         functools.partial(unpack_kernel, factor),
         out_shape=(jax.ShapeDtypeStruct((256, 128), F32), shape, shape, shape),
         in_specs=[vmem] * 2,
-        out_specs=(vmem,) * 4,
+        out_specs=(hbm,) * 4,
+        scratch_shapes=[pltpu.VMEM(k1.shape, F32)] * 3 + [dma((4,))],
+        compiler_params=pltpu.CompilerParams(vmem_limit_bytes=8 * 1024 * 1024),
         name="unpack",
     )(gin, red.reshape(3, 256, 128))
     return gin.reshape(x1.shape), out1, out2, out3

time: 49.8 us -> 46.7 us (0.938)
  Pallas kernels: 49 us -> 46 us
    pallas_call x1, Pallas kernels: 46.6 us -> 44.6 us  [per_device(): pl.pallas_call(functools.partial(step_kernel, dims), out_shape=(jax.Shape...]
    pallas_call x1, Pallas kernels: 2.41 us -> 1.33 us  [per_device(): pl.pallas_call(functools.partial(unpack_kernel, factor), out_shape=(jax.S...]
where the time goes in v2:
time: 46.7 us; the launch traced here: 46.6 us
  Pallas kernels  46 us (99%)
  between operations  0.64 us (1%)
    pallas_call x1, Pallas kernels, per_device(): pl.pallas_call(functools.partial(step_kernel, dims), out_shape=(jax.Shape...  44.6 us
    pallas_call x1, Pallas kernels, per_device(): pl.pallas_call(functools.partial(unpack_kernel, factor), out_shape=(jax.S...  1.33 us

profile of v2, /device:TPU:1, one launch (start us, length us, event | category | flops | bytes accessed | tf_op | source)
XLA Modules:
  0.0 46.6 jit_solution(16140684490887710380)
XLA Ops:
  0.6 44.6 %step.1 = (f32[256,128]{1,0:T(8,128)S(1)}, f32[3,32,8,128]{3,2,1,0:T(8,128)S(1)}) custom-call(f32[256,128]{1,0:T(8,128)} %bitcast.7, f32[256,128]{1,0:T(8,128)} %bitcast.8, f32[256,128]{1,0:T(8,128)} %bitcast.9, f32[256,128]{1,0:T(8,128)} %bitcast.10, f32[27,32,32]{2,1,0:T(8,128)} %k3_in.1, f32[27,32,32]{2,1,0:T(8,128)} %k2_in.1, f32[27,32,32]{2,1,0:T(8,128)} %k1_in.1), custom_call_target="tpu_custom_call" | custom-call | tf_op jit(solution)/shard_map/step/pallas_call | solution.py:430
  45.3 1.3 %unpack.1 = (f32[256,128]{1,0:T(8,128)}, f32[27,32,32]{2,1,0:T(8,128)}, f32[27,32,32]{2,1,0:T(8,128)}, f32[27,32,32]{2,1,0:T(8,128)}) custom-call(f32[256,128]{1,0:T(8,128)S(1)} %get-tuple-element.10.gin_in, f32[3,256,128]{2,1,0:T(8,128)S(1)} %bitcast.6), custom_call_target="tpu_custom_call" | custom-call | tf_op jit(solution)/shard_map/unpack/pallas_call | solution.py:457

commit v3 on v2

--- a/solution.py
+++ b/solution.py
@@ -51,14 +51,29 @@
     core, my_z, my_y = lax.rem(gx, 2), lax.rem(lax.div(gx, 2), zn), lax.div(gx, 2 * zn)
     me = (my_y * 2 + core) * gyn + gy
 
-    lines = []
-    for ky in range(ylo):
-        for kc in range(2):
-            other_y, other_core = lax.rem(my_y + ky, ylo), lax.rem(core + kc, 2)
-            lines.append((other_y * (2 * zn) + my_z * 2 + other_core, (other_y * 2 + other_core) * gyn))
-    spots = [lax.rem(gy + k, gyn) for k in range(gyn)]
-    peers = [((at, spot), base + spot) for spot in spots for at, base in lines][1:]
-    z_peers = [(my_y * (2 * zn) + lax.rem(my_z + k, zn) * 2 + core, gy) for k in range(1, zn)]
+    xs = min(4, gyn)
+    yhi = gyn // xs
+    my_x, my_yhi = lax.rem(gy, xs), lax.div(gy, xs)
+    cores = [lax.rem(core + k, 2) for k in range(2)]
+    lows = [lax.rem(my_y + k, ylo) for k in range(ylo)]
+    highs = [lax.rem(my_yhi + k, yhi) for k in range(yhi)]
+    columns = [lax.rem(my_x + k, xs) for k in range(xs)]
+    order = []
+    for kc in range(2):
+        for kl in range(ylo):
+            for kh in range(yhi):
+                for kx in range(xs):
+                    hops = min(kx, xs - kx) + (1 if kl else 2 * kh)
+                    order.append((-hops, kc, kl, kh, kx))
+    peers = []
+    for _, kc, kl, kh, kx in sorted(order):
+        if kc or kl or kh or kx:
+            spot = highs[kh] * xs + columns[kx]
+            line = lows[kl] * 2 + cores[kc]
+            at = lows[kl] * (2 * zn) + my_z * 2 + cores[kc]
+            peers.append(((at, spot), line * gyn + spot))
+    z_order = sorted(range(1, zn), key=lambda k: -min(k, zn - k))
+    z_peers = [(my_y * (2 * zn) + lax.rem(my_z + k, zn) * 2 + core, gy) for k in z_order]
 
     def near(n, side):
         return (lax.rem(gx + n + gxn, gxn), lax.rem(gy + side + gyn, gyn))
@@ -73,7 +88,7 @@
 
     barrier = pltpu.get_barrier_semaphore()
     around = [near(n, s) for n, s in SIDES] + [near(-1, 0), near(1, 0)]
-    greeted = around + [device for device, _ in peers] + z_peers
+    greeted = z_peers + [device for device, _ in peers] + around
     for device in greeted:
         pl.semaphore_signal(barrier, inc=1, device_id=device, device_id_type=MESH)
 
@@ -368,6 +383,10 @@
             fill_own(3, h)
             kernel_grad(layer, layer, h, packed)
             rs_start(layer)
+            if layer > 0:
+                z_start(layer - 1)
+            if layer == 2:
+                ag_start(0)
             if layer < 2:
                 build_weights(layer + 1, (k2, k1)[layer])
                 halo_wait(layer + 1)
@@ -380,15 +399,11 @@
             halo_wait(3 + layer)
             fill_halo(3, 3 + layer)
             grad = conv(3 + layer, 3)
-            if layer == 1:
-                z_start(0)
         for z in range(2):
             for x in range(4):
                 gin_ref[pl.ds(z * 4 + x, 32, stride=8), :] = grad[z][x]
-        z_start(1)
-        ag_start(0)
+        ag_start(1)
         z_start(2)
-        ag_start(1)
         finish(0)
         ag_start(2)
         finish(1)

time: 46.7 us -> 46.2 us (0.989)
  Pallas kernels: 46 us -> 45.5 us
    pallas_call x1, Pallas kernels: 44.6 us -> 44.1 us  [per_device(): pl.pallas_call(functools.partial(step_kernel, dims), out_shape=(jax.Shape...]
where the time goes in v3:
time: 46.2 us; the launch traced here: 46.1 us
  Pallas kernels  45.5 us (98%)
  between operations  0.64 us (1%)
    pallas_call x1, Pallas kernels, per_device(): pl.pallas_call(functools.partial(step_kernel, dims), out_shape=(jax.Shape...  44.1 us
    pallas_call x1, Pallas kernels, per_device(): pl.pallas_call(functools.partial(unpack_kernel, factor), out_shape=(jax.S...  1.33 us

profile of v3, /device:TPU:1, one launch (start us, length us, event | category | flops | bytes accessed | tf_op | source)
XLA Modules:
  0.0 46.1 jit_solution(245834632604192365)
XLA Ops:
  0.6 44.1 %step.1 = (f32[256,128]{1,0:T(8,128)S(1)}, f32[3,32,8,128]{3,2,1,0:T(8,128)S(1)}) custom-call(f32[256,128]{1,0:T(8,128)} %bitcast.7, f32[256,128]{1,0:T(8,128)} %bitcast.8, f32[256,128]{1,0:T(8,128)} %bitcast.9, f32[256,128]{1,0:T(8,128)} %bitcast.10, f32[27,32,32]{2,1,0:T(8,128)} %k3_in.1, f32[27,32,32]{2,1,0:T(8,128)} %k2_in.1, f32[27,32,32]{2,1,0:T(8,128)} %k1_in.1), custom_call_target="tpu_custom_call" | custom-call | tf_op jit(solution)/shard_map/step/pallas_call | solution.py:445
  44.8 1.3 %unpack.1 = (f32[256,128]{1,0:T(8,128)}, f32[27,32,32]{2,1,0:T(8,128)}, f32[27,32,32]{2,1,0:T(8,128)}, f32[27,32,32]{2,1,0:T(8,128)}) custom-call(f32[256,128]{1,0:T(8,128)S(1)} %get-tuple-element.10.gin_in, f32[3,256,128]{2,1,0:T(8,128)S(1)} %bitcast.6), custom_call_target="tpu_custom_call" | custom-call | tf_op jit(solution)/shard_map/unpack/pallas_call | solution.py:472

commit v4 on v3

--- a/solution.py
+++ b/solution.py
@@ -36,11 +36,15 @@
     return lax.broadcasted_iota(jnp.int32, (rows, 128), 1)
 
 
+def tile_of(row):
+    return row if 0 <= row < 4 else (5 - 2 * (row + 1) if row < 0 else 6 + 2 * (row - 4))
+
+
 def step_kernel(
     dims, x3_in, cot_in, x2_in, x1_in, k3_in, k2_in, k1_in,
     gin_ref, red_ref,
     x3, cot, x2, x1, k3, k2, k1,
-    send, recv, field, weights, hmat, prod, slope,
+    send, recv, field, weights, hmat, prod, held,
     part, rs_recv, z_recv, ag_recv,
     load_sem, halo_send, halo_recv, rs_send_sem, rs_recv_sem, z_send_sem, z_recv_sem, ag_send_sem, ag_recv_sem,
 ):
@@ -99,105 +103,120 @@
     lane8, lane32 = lanes(8), lanes(32)
     zero32 = jnp.zeros((32, 128), F32)
 
-    for bi in range(4):
-        for part_row in (0, 256):
-            for z in range(2):
-                base = part_row + z * 128 + 96
-                field[bi, base : base + 32, :] = jnp.zeros((32, 640), BF16)
+    spot8, spot32 = lane8 % 8, lane32 % 8
+    outside = jnp.where(spot8 < 3, left, jnp.where(spot8 >= 5, right, 1.0))
+    outside = outside * jnp.where(lane8 < 24, up, jnp.where(lane8 >= 56, down, 1.0))
+    outside = jnp.concatenate([outside] * 4, axis=0)
+
+    def clear_padding():
+        for bi in range(6):
+            width = 128 * (9, 7, 5, 7, 5, 5)[bi]
+            for base in (96, 224, 352, 480):
+                field[bi, base : base + 32, 0:width] = jnp.zeros((32, width), BF16)
 
     def load_tiles(ref):
-        return [[ref[pl.ds(z * 4 + x, 32, stride=8), :] for x in range(4)] for z in range(2)]
+        return [{x: ref[pl.ds(z * 4 + x, 32, stride=8), :] for x in range(4)} for z in range(2)]
 
     def edge_columns(tiles):
         packed = []
         for z in range(2):
             total = zero32
-            for x in range(4):
-                keep = (lane32 == 8 * x) | (lane32 == (8 * x - 1) % 128)
-                total = jnp.where(keep, roll(tiles[z][x], 8 * x), total)
+            for row, tile in tiles[z].items():
+                base = 8 * (row + 3)
+                total = jnp.where((lane32 >= base + 2) & (lane32 < base + 8), roll(tile, base + 5), total)
             packed.append(total)
         return packed
 
     def fill_send(f, tiles, packed):
         for z in range(2):
-            send[f, z * 32 : z * 32 + 32, :] = tiles[z][0]
-            send[f, 64 + z * 32 : 96 + z * 32, :] = tiles[z][3]
-        squeezed = None
-        for z in range(2):
+            squeezed = None
             for v in range(4):
-                term = roll(packed[z][8 * v : 8 * v + 8], 2 * v + 64 * z)
+                term = roll(packed[z][8 * v : 8 * v + 8], 32 * v - 24)
                 squeezed = term if squeezed is None else squeezed + term
-        send[f, 128:136, :] = squeezed
-
-    def fill_own(bi, tiles):
-        for z in range(2):
-            for x_in in range(4):
-                high, low = split(tiles[z][x_in])
+            send[f, 256 + 8 * z : 264 + 8 * z, :] = squeezed
+        for z in range(2):
+            for x in range(4):
+                send[f, x * 64 + z * 32 : x * 64 + z * 32 + 32, :] = tiles[z][x]
+
+    def fill_rows(bi, extent, tiles):
+        for z in range(2):
+            for row_in, tile in tiles[z].items():
+                high, low = split(tile)
                 for b in range(3):
-                    x = x_in + 1 - b
-                    if 0 <= x < 4:
-                        row, col = z * 128 + b * 32, x * 128
+                    row_out = row_in + 1 - b
+                    if -extent <= row_out < 4 + extent:
+                        row, col = z * 128 + b * 32, tile_of(row_out) * 128
                         field[bi, row : row + 32, col : col + 128] = high
                         field[bi, 256 + row : 288 + row, col : col + 128] = low
 
-    def halo_copies(f):
-        copies = []
-
-        def add(lo, hi, at, device):
-            copies.append(
-                pltpu.make_async_remote_copy(
-                    src_ref=send.at[f, pl.ds(lo, hi - lo)],
-                    dst_ref=recv.at[f, pl.ds(at, hi - lo)],
-                    send_sem=halo_send.at[f],
-                    recv_sem=halo_recv.at[f],
-                    device_id=device,
-                    device_id_type=MESH,
-                )
-            )
-
-        for k, (n, s) in enumerate(SIDES):
-            add(128, 136, 128 + 8 * k, near(-n, -s))
-        add(64, 128, 0, near(1, 0))
-        add(0, 64, 64, near(-1, 0))
-        return copies
-
-    def start_halo(f):
-        for copy in halo_copies(f):
-            copy.start()
-
-    def whole_halo(f):
-        return pltpu.make_async_remote_copy(
-            src_ref=recv.at[f], dst_ref=recv.at[f], send_sem=halo_send.at[f], recv_sem=halo_recv.at[f],
-            device_id=near(1, 0), device_id_type=MESH,
-        )
-
-    def halo_wait(f):
-        whole_halo(f).wait_recv()
-
-    def fill_halo(bi, f):
-        for z in range(2):
-            for at, b, x, ok in ((0, 0, 0, up), (64, 2, 3, down)):
-                high, low = split(recv[f, at + z * 32 : at + z * 32 + 32, :] * ok)
-                row, col = z * 128 + b * 32, x * 128
-                field[bi, row : row + 32, col : col + 128] = high
-                field[bi, 256 + row : 288 + row, col : col + 128] = low
-        first = ((lane8 & 63) >= 55) & ((lane8 & 63) <= 62)
-        last = ((lane8 & 63) >= 31) & ((lane8 & 63) <= 38)
-        merged = []
-        for k, ok in ((0, left), (3, right)):
-            tile = [recv[f, 128 + 8 * (k + j) : 136 + 8 * (k + j), :] for j in range(3)]
-            total = tile[1]
-            total = total + jnp.where(first, roll(tile[0], 96), 0.0) * up
-            total = total + jnp.where(last, roll(tile[2], 32), 0.0) * down
-            merged.append(total * ok)
-        both = jnp.where(lane8 % 2 == 1, roll(merged[0], 2), merged[1])
+    def fill_edges(bi, edges):
         for z in range(2):
             for b in range(3):
-                tile = jnp.concatenate([roll(both, 7 - 2 * v - 64 * z - 8 * b) for v in range(4)], axis=0)
-                high, low = split(tile)
+                high, low = split(roll(edges[z], 8 - 8 * b))
                 row = z * 128 + b * 32
                 field[bi, row : row + 32, 512:640] = high
                 field[bi, 256 + row : 288 + row, 512:640] = low
+
+    def own_edges(packed, other):
+        return [
+            jnp.where(spot32 == 4, packed[z], jnp.where(spot32 == 3, roll(packed[z], -2), other[z]))
+            for z in range(2)
+        ]
+
+    depth = (3, 2, 2, 1, 1)
+
+    def start_halo(f):
+        d = depth[f] * 64
+
+        def go(src, dst, rows, device):
+            pltpu.make_async_remote_copy(
+                src_ref=send.at[f, pl.ds(src, rows)],
+                dst_ref=recv.at[f, pl.ds(dst, rows)],
+                send_sem=halo_send.at[f],
+                recv_sem=halo_recv.at[f],
+                device_id=device,
+                device_id_type=MESH,
+            ).start()
+
+        for k in (0, 2, 3, 5, 1, 4):
+            go(256, 2 * d + 16 * k, 16, near(-SIDES[k][0], -SIDES[k][1]))
+        go(256 - d, 0, d, near(1, 0))
+        go(0, d, d, near(-1, 0))
+
+    def whole_halo(f):
+        ref = recv.at[f, pl.ds(0, 128 * depth[f] + 96)]
+        return pltpu.make_async_remote_copy(
+            src_ref=ref, dst_ref=ref, send_sem=halo_send.at[f], recv_sem=halo_recv.at[f],
+            device_id=near(1, 0), device_id_type=MESH,
+        )
+
+    def halo_rows(f):
+        d = depth[f]
+        rows = [{}, {}]
+        for z in range(2):
+            for i in range(d):
+                at = i * 64 + z * 32
+                rows[z][i - d] = recv[f, at : at + 32, :] * up
+                rows[z][4 + i] = recv[f, d * 64 + at : d * 64 + at + 32, :] * down
+        return rows
+
+    def halo_edges(f):
+        base = 128 * depth[f]
+        edges = []
+        for z in range(2):
+            merged = []
+            for j, ok in ((0, up), (1, None), (2, down)):
+                at = base + 16 * j + 8 * z
+                near_left, near_right = recv[f, at : at + 8, :], recv[f, at + 48 : at + 56, :]
+                tile = jnp.where(spot8 < 3, roll(near_left, -2) * left, jnp.where(spot8 >= 5, near_right * right, 0.0))
+                merged.append(tile if ok is None else tile * ok)
+            tiles = []
+            for v in range(4):
+                tile = jnp.where(lane8 < 24, roll(merged[0], -8 - 32 * v), roll(merged[1], 24 - 32 * v))
+                tile = jnp.where(lane8 >= 56, roll(merged[2], 56 - 32 * v), tile)
+                tiles.append(jnp.where(lane8 < 88, tile, 0.0))
+            edges.append(jnp.concatenate(tiles, axis=0))
+        return edges
 
     def row_block(kernel, a, c):
         return jnp.concatenate(
@@ -229,30 +248,33 @@
                         store_weights(layer, c * 64 + z * 32, zp * 128, blocks[c])
                         store_weights(3 + layer, c * 64 + zp * 32, z * 128, back)
 
-    def conv(wi, bi):
-        for lo, hi in ((0, 256), (256, 512), (512, 640)):
+    def conv(wi, bi, extent):
+        width = 128 * (5 + 2 * extent)
+        for lo in range(0, width, 256):
+            hi = min(lo + 256, width)
             prod[:, lo:hi] = jnp.dot(
                 weights[wi, :, 0:512], field[bi, :, lo:hi], preferred_element_type=F32
             ) + jnp.dot(weights[wi, :, 512:768], field[bi, 0:256, lo:hi], preferred_element_type=F32)
-        out = []
+        out, edges = [], []
         for z in range(2):
             row = z * 32
-            edge = jnp.where(
-                lane32 % 8 == 0, prod[row : row + 32, 512:640], prod[128 + row : 160 + row, 512:640]
-            )
-            tiles = []
-            for x in range(4):
-                col = x * 128
-                at_edge = roll(edge, -8 * x)
+            p0, p1, p2 = (prod[c * 64 + row : c * 64 + row + 32, 512:640] for c in range(3))
+            edge = jnp.where(spot32 == 2, p0, roll(p2, -4))
+            if extent:
+                edges.append(p1 + roll(p0, 1) + roll(p2, -1))
+            tiles = {}
+            for x in range(-extent, 4 + extent):
+                col = tile_of(x) * 128
+                at_edge = roll(edge, -8 * (x + 3) - 2)
                 before = roll(prod[row : row + 32, col : col + 128], 1)
                 after = roll(prod[128 + row : 160 + row, col : col + 128], -1)
-                tiles.append(
+                tiles[x] = (
                     prod[64 + row : 96 + row, col : col + 128]
                     + jnp.where(lane32 == 0, at_edge, before)
                     + jnp.where(lane32 == 127, at_edge, after)
                 )
             out.append(tiles)
-        return out
+        return out, edges
 
     def store_h(c, z, col, tile):
         high, low = split(tile)
@@ -260,19 +282,30 @@
         hmat[row : row + 32, col : col + 128] = high
         hmat[192 + row : 224 + row, col : col + 128] = low
 
-    def kernel_grad(layer, bi, tiles, packed):
+    def keep_h(layer, tiles, packed):
         for z in range(2):
             for x in range(4):
-                col = x * 128
-                store_h(0, z, col, jnp.where(lane32 == 127, 0.0, roll(tiles[z][x], -1)))
-                store_h(1, z, col, tiles[z][x])
-                store_h(2, z, col, jnp.where(lane32 == 0, 0.0, roll(tiles[z][x], 1)))
-            store_h(0, z, 512, jnp.where(lane32 % 8 == 0, packed[z], 0.0))
+                at = (z * 5 + x) * 32
+                held[layer, at : at + 32, :] = tiles[z][x]
+            held[layer, z * 160 + 128 : z * 160 + 160, :] = packed[z]
+
+    def kernel_grad(layer):
+        bi = layer
+        own = (lane32 >= 24) & (lane32 < 56)
+        for z in range(2):
+            for x in range(4):
+                col, at = x * 128, (z * 5 + x) * 32
+                tile = held[layer, at : at + 32, :]
+                store_h(0, z, col, jnp.where(lane32 == 127, 0.0, roll(tile, -1)))
+                store_h(1, z, col, tile)
+                store_h(2, z, col, jnp.where(lane32 == 0, 0.0, roll(tile, 1)))
+            packed = held[layer, z * 160 + 128 : z * 160 + 160, :]
+            store_h(0, z, 512, jnp.where(own & (spot32 == 2), roll(packed, -3), 0.0))
             store_h(1, z, 512, zero32)
-            store_h(2, z, 512, jnp.where(lane32 % 8 == 7, packed[z], 0.0))
+            store_h(2, z, 512, jnp.where(own & (spot32 == 5), roll(packed, 1), 0.0))
         contract = (((1,), (1,)), ((), ()))
-        main = lax.dot_general(hmat[...], field[bi, 0:256, :], contract, preferred_element_type=F32)
-        rest = lax.dot_general(hmat[0:192, :], field[bi, 256:512, :], contract, preferred_element_type=F32)
+        main = lax.dot_general(hmat[...], field[bi, 0:256, 0:640], contract, preferred_element_type=F32)
+        rest = lax.dot_general(hmat[0:192, :], field[bi, 256:512, 0:640], contract, preferred_element_type=F32)
         total = main[0:192] + main[192:384] + rest
         blocks = []
         for c in range(3):
@@ -348,67 +381,93 @@
 
     def sequence():
         loads[0].wait()
-        tiles = load_tiles(x3)
-        fill_send(0, tiles, edge_columns(tiles))
+        tiles3 = load_tiles(x3)
+        packed3 = edge_columns(tiles3)
+        fill_send(0, tiles3, packed3)
         pl.semaphore_wait(barrier, len(greeted))
         start_halo(0)
-        fill_own(0, tiles)
-        for f, ref, at in ((1, x2, 3), (2, x1, 4)):
+        zero = [zero32, zero32]
+        for f, ref, at in ((1, cot, 2), (2, x2, 3), (3, x1, 4)):
             loads[at].wait()
             tiles = load_tiles(ref)
-            fill_send(f, tiles, edge_columns(tiles))
+            packed = edge_columns(tiles)
+            fill_send(f, tiles, packed)
             start_halo(f)
-            fill_own(f, tiles)
-        loads[1].wait()
-        build_weights(0, k3)
-        loads[2].wait()
-        loads[5].wait()
-        loads[6].wait()
-        grad = load_tiles(cot)
-
-        for layer in range(3):
-            if layer == 0:
-                halo_wait(0)
-                fill_halo(0, 0)
-                pre = conv(0, 0)
-                mult = [[gelu_slope(pre[z][x]) for x in range(4)] for z in range(2)]
-            else:
-                mult = [
-                    [slope[layer - 1, (z * 4 + x) * 32 : (z * 4 + x) * 32 + 32, :] for x in range(4)] for z in range(2)
-                ]
-            h = [[grad[z][x] * mult[z][x] for x in range(4)] for z in range(2)]
-            packed = edge_columns(h)
-            fill_send(3 + layer, h, packed)
-            start_halo(3 + layer)
-            fill_own(3, h)
-            kernel_grad(layer, layer, h, packed)
-            rs_start(layer)
-            if layer > 0:
-                z_start(layer - 1)
-            if layer == 2:
-                ag_start(0)
-            if layer < 2:
-                build_weights(layer + 1, (k2, k1)[layer])
-                halo_wait(layer + 1)
-                fill_halo(layer + 1, layer + 1)
-                pre = conv(layer + 1, layer + 1)
-                for z in range(2):
-                    for x in range(4):
-                        at = (z * 4 + x) * 32
-                        slope[layer, at : at + 32, :] = gelu_slope(pre[z][x])
-            halo_wait(3 + layer)
-            fill_halo(3, 3 + layer)
-            grad = conv(3 + layer, 3)
+            if f > 1:
+                fill_rows(f - 1, 3 - f, tiles)
+        clear_padding()
+        fill_rows(0, 2, tiles3)
+        for at, kernel, layer in ((1, k3, 0), (5, k2, 1), (6, k1, 2)):
+            loads[at].wait()
+            build_weights(layer, kernel)
+
+        def forward(layer, f, extent, ref):
+            near_packed = edge_columns(load_tiles(ref)) if extent else zero
+            whole_halo(f).wait_recv()
+            rows, edges = halo_rows(f), halo_edges(f)
+            fill_rows(layer, extent, rows)
+            if extent:
+                far_packed = edge_columns(rows)
+                edges = own_edges([near_packed[z] + far_packed[z] for z in range(2)], edges)
+            fill_edges(layer, edges)
+            return conv(layer, layer, extent)
+
+        pre, pre_edge = forward(0, 0, 2, x3)
+        whole_halo(1).wait_recv()
+        grad, far = load_tiles(cot), halo_rows(1)
+        h = []
+        for z in range(2):
+            grad[z].update(far[z])
+            h.append({x: grad[z][x] * gelu_slope(pre[z][x]) for x in range(-2, 6)})
+        grad_edge = halo_edges(1)
+        packed = edge_columns(h)
+        keep_h(0, h, packed)
+        fill_rows(3, 1, h)
+        fill_edges(3, own_edges(packed, [grad_edge[z] * gelu_slope(pre_edge[z]) for z in range(2)]))
+        grad, grad_edge = conv(3, 3, 1)
+
+        pre, pre_edge = forward(1, 2, 1, x2)
+        h = []
+        for z in range(2):
+            h.append({x: grad[z][x] * gelu_slope(pre[z][x]) for x in range(-1, 5)})
+            h[z][-1] = h[z][-1] * up
+            h[z][4] = h[z][4] * down
+        packed = edge_columns(h)
+        keep_h(1, h, packed)
+        fill_rows(4, 0, h)
+        fill_edges(4, [grad_edge[z] * gelu_slope(pre_edge[z]) * outside for z in range(2)])
+        grad, _ = conv(4, 4, 0)
+
+        pre, _ = forward(2, 3, 0, x1)
+        h = [{x: grad[z][x] * gelu_slope(pre[z][x]) for x in range(4)} for z in range(2)]
+        packed = edge_columns(h)
+        fill_send(4, h, packed)
+        start_halo(4)
+        keep_h(2, h, packed)
+        kernel_grad(2)
+        rs_start(2)
+        kernel_grad(0)
+        rs_start(0)
+        kernel_grad(1)
+        rs_start(1)
+        fill_rows(5, 0, h)
+        whole_halo(4).wait_recv()
+        fill_rows(5, 0, halo_rows(4))
+        fill_edges(5, halo_edges(4))
+        grad, _ = conv(5, 5, 0)
         for z in range(2):
             for x in range(4):
                 gin_ref[pl.ds(z * 4 + x, 32, stride=8), :] = grad[z][x]
+        z_start(2)
+        z_start(0)
+        z_start(1)
+        ag_start(2)
+        ag_start(0)
         ag_start(1)
-        z_start(2)
+        finish(2)
         finish(0)
-        ag_start(2)
         finish(1)
-        finish(2)
-        for f in range(6):
+        for f in range(5):
             whole_halo(f).wait_send()
         for layer in range(3):
             rs_wait(layer).wait_send()
@@ -450,18 +509,18 @@
         scratch_shapes=[pltpu.VMEM((256, 128), F32)] * 4
         + [pltpu.VMEM((27, 32, 32), F32)] * 3
         + [
-            pltpu.VMEM((6, 136, 128), F32),
-            pltpu.VMEM((6, 176, 128), F32),
-            pltpu.VMEM((4, 512, 640), BF16),
+            pltpu.VMEM((5, 272, 128), F32),
+            pltpu.VMEM((5, 480, 128), F32),
+            pltpu.VMEM((6, 512, 1152), BF16),
             pltpu.VMEM((6, 192, 768), BF16),
             pltpu.VMEM((384, 640), BF16),
-            pltpu.VMEM((192, 640), F32),
-            pltpu.VMEM((2, 256, 128), F32),
+            pltpu.VMEM((192, 1152), F32),
+            pltpu.VMEM((3, 320, 128), F32),
             pltpu.VMEM((3, 32, 8, 128), F32),
             pltpu.VMEM((3, 32, 8, 128), F32),
             pltpu.VMEM((3, dims[2], per, 8, 128), F32),
             pltpu.VMEM((3, 32, 8, 128), F32),
-            dma((7,)), dma((6,)), dma((6,)), dma((3,)), dma((3,)), dma((3,)), dma((3,)), dma((3,)), dma((3,)),
+            dma((7,)), dma((5,)), dma((5,)), dma((3,)), dma((3,)), dma((3,)), dma((3,)), dma((3,)), dma((3,)),
         ],
         compiler_params=pltpu.CompilerParams(
             collective_id=0, has_side_effects=True, vmem_limit_bytes=40 * 1024 * 1024

time: 46.2 us -> 41.2 us (0.89)
  Pallas kernels: 45.5 us -> 40.4 us
    pallas_call x1, Pallas kernels: 44.1 us -> 39.1 us  [per_device(): pl.pallas_call(functools.partial(step_kernel, dims), out_shape=(jax.Shape...]
where the time goes in v4:
time: 41.2 us; the launch traced here: 41.1 us
  Pallas kernels  40.4 us (98%)
  between operations  0.64 us (2%)
    pallas_call x1, Pallas kernels, per_device(): pl.pallas_call(functools.partial(step_kernel, dims), out_shape=(jax.Shape...  39.1 us
    pallas_call x1, Pallas kernels, per_device(): pl.pallas_call(functools.partial(unpack_kernel, factor), out_shape=(jax.S...  1.33 us

profile of v4, /device:TPU:1, one launch (start us, length us, event | category | flops | bytes accessed | tf_op | source)
XLA Modules:
  0.0 41.1 jit_solution(3038567919512968002)
XLA Ops:
  0.6 39.1 %step.1 = (f32[256,128]{1,0:T(8,128)S(1)}, f32[3,32,8,128]{3,2,1,0:T(8,128)S(1)}) custom-call(f32[256,128]{1,0:T(8,128)} %bitcast.7, f32[256,128]{1,0:T(8,128)} %bitcast.8, f32[256,128]{1,0:T(8,128)} %bitcast.9, f32[256,128]{1,0:T(8,128)} %bitcast.10, f32[27,32,32]{2,1,0:T(8,128)} %k3_in.1, f32[27,32,32]{2,1,0:T(8,128)} %k2_in.1, f32[27,32,32]{2,1,0:T(8,128)} %k1_in.1), custom_call_target="tpu_custom_call" | custom-call | tf_op jit(solution)/shard_map/step/pallas_call | solution.py:504
  39.7 1.3 %unpack.1 = (f32[256,128]{1,0:T(8,128)}, f32[27,32,32]{2,1,0:T(8,128)}, f32[27,32,32]{2,1,0:T(8,128)}, f32[27,32,32]{2,1,0:T(8,128)}) custom-call(f32[256,128]{1,0:T(8,128)S(1)} %get-tuple-element.10.gin_in, f32[3,256,128]{2,1,0:T(8,128)S(1)} %bitcast.6), custom_call_target="tpu_custom_call" | custom-call | tf_op jit(solution)/shard_map/unpack/pallas_call | solution.py:531

commit v5 on v4

--- a/solution.py
+++ b/solution.py
@@ -37,7 +37,7 @@
 
 
 def tile_of(row):
-    return row if 0 <= row < 4 else (5 - 2 * (row + 1) if row < 0 else 6 + 2 * (row - 4))
+    return (1, 2, 0, 3, None, -1, 4, -2, 5).index(row)
 
 
 def step_kernel(
@@ -50,7 +50,6 @@
 ):
     gxn, gyn, zn, ylo = dims
     members = ylo * 2 * gyn
-    per = 32 // members
     gx, gy = lax.axis_index("gx"), lax.axis_index("gy")
     core, my_z, my_y = lax.rem(gx, 2), lax.rem(lax.div(gx, 2), zn), lax.div(gx, 2 * zn)
     me = (my_y * 2 + core) * gyn + gy
@@ -69,15 +68,26 @@
                 for kx in range(xs):
                     hops = min(kx, xs - kx) + (1 if kl else 2 * kh)
                     order.append((-hops, kc, kl, kh, kx))
-    peers = []
+    peers, alike = [], []
     for _, kc, kl, kh, kx in sorted(order):
         if kc or kl or kh or kx:
             spot = highs[kh] * xs + columns[kx]
             line = lows[kl] * 2 + cores[kc]
             at = lows[kl] * (2 * zn) + my_z * 2 + cores[kc]
             peers.append(((at, spot), line * gyn + spot))
+            if kc == 0:
+                alike.append((at, spot))
     z_order = sorted(range(1, zn), key=lambda k: -min(k, zn - k))
     z_peers = [(my_y * (2 * zn) + lax.rem(my_z + k, zn) * 2 + core, gy) for k in z_order]
+
+    line_peers = []
+    for _, kz, kc in sorted((-min(k, zn - k), k, c) for k in range(zn) for c in range(2)):
+        if kz or kc:
+            at_z = lax.rem(my_z + kz, zn)
+            line_peers.append(((my_y * (2 * zn) + at_z * 2 + cores[kc], gy), cores[kc] * zn + at_z))
+    plane = (peers, me, members, z_peers, my_z, zn)
+    column = (line_peers, core * zn + my_z, 2 * zn, alike, my_y * gyn + gy, ylo * gyn)
+    plans = [column if layer in (0,) else plane for layer in range(3)]
 
     def near(n, side):
         return (lax.rem(gx + n + gxn, gxn), lax.rem(gy + side + gyn, gyn))
@@ -92,7 +102,7 @@
 
     barrier = pltpu.get_barrier_semaphore()
     around = [near(n, s) for n, s in SIDES] + [near(-1, 0), near(1, 0)]
-    greeted = z_peers + [device for device, _ in peers] + around
+    greeted = [device for device, _ in line_peers] + [device for device, _ in peers] + around
     for device in greeted:
         pl.semaphore_signal(barrier, inc=1, device_id=device, device_id_type=MESH)
 
@@ -127,16 +137,30 @@
             packed.append(total)
         return packed
 
-    def fill_send(f, tiles, packed):
-        for z in range(2):
-            squeezed = None
-            for v in range(4):
-                term = roll(packed[z][8 * v : 8 * v + 8], 32 * v - 24)
-                squeezed = term if squeezed is None else squeezed + term
-            send[f, 256 + 8 * z : 264 + 8 * z, :] = squeezed
+    depth = (3, 2, 2, 1, 1)
+    riders = {0: ((0, 2, 5), (3, 0, 1)), 1: ((1, 0, 2), (2, 4, 6)), 4: ((4, 0, 1),)}
+
+    def fill_send(f, tiles):
         for z in range(2):
             for x in range(4):
                 send[f, x * 64 + z * 32 : x * 64 + z * 32 + 32, :] = tiles[z][x]
+
+    def within(start, size):
+        return (spot8 >= start) & (spot8 < start + size)
+
+    def fill_columns(f, packs):
+        to_right = to_left = jnp.zeros((8, 128), F32)
+        for g, *targets in riders[f]:
+            d = depth[g]
+            for z, t in enumerate(targets):
+                squeezed = None
+                for v in range(4):
+                    term = roll(packs[g][z][8 * v : 8 * v + 8], 32 * v - 24)
+                    squeezed = term if squeezed is None else squeezed + term
+                to_right = jnp.where(within(t, d), roll(squeezed, t - 5 + d), to_right)
+                to_left = jnp.where(within(t, d), roll(squeezed, t - 5), to_left)
+        send[f, 256:264, :] = to_right
+        send[f, 264:272, :] = to_left
 
     def fill_rows(bi, extent, tiles):
         for z in range(2):
@@ -162,8 +186,6 @@
             jnp.where(spot32 == 4, packed[z], jnp.where(spot32 == 3, roll(packed[z], -2), other[z]))
             for z in range(2)
         ]
-
-    depth = (3, 2, 2, 1, 1)
 
     def start_halo(f):
         d = depth[f] * 64
@@ -178,13 +200,14 @@
                 device_id_type=MESH,
             ).start()
 
-        for k in (0, 2, 3, 5, 1, 4):
-            go(256, 2 * d + 16 * k, 16, near(-SIDES[k][0], -SIDES[k][1]))
+        if f in riders:
+            for k in (0, 2, 3, 5, 1, 4):
+                go(256 if k < 3 else 264, 2 * d + 8 * k, 8, near(-SIDES[k][0], -SIDES[k][1]))
         go(256 - d, 0, d, near(1, 0))
         go(0, d, d, near(-1, 0))
 
     def whole_halo(f):
-        ref = recv.at[f, pl.ds(0, 128 * depth[f] + 96)]
+        ref = recv.at[f, pl.ds(0, 128 * depth[f] + (48 if f in riders else 0))]
         return pltpu.make_async_remote_copy(
             src_ref=ref, dst_ref=ref, send_sem=halo_send.at[f], recv_sem=halo_recv.at[f],
             device_id=near(1, 0), device_id_type=MESH,
@@ -201,14 +224,17 @@
         return rows
 
     def halo_edges(f):
-        base = 128 * depth[f]
+        carrier = {3: 0, 2: 1}.get(f, f)
+        base, d = 128 * depth[carrier], depth[f]
+        targets = [rider[1:] for rider in riders[carrier] if rider[0] == f][0]
         edges = []
-        for z in range(2):
+        for t in targets:
             merged = []
             for j, ok in ((0, up), (1, None), (2, down)):
-                at = base + 16 * j + 8 * z
-                near_left, near_right = recv[f, at : at + 8, :], recv[f, at + 48 : at + 56, :]
-                tile = jnp.where(spot8 < 3, roll(near_left, -2) * left, jnp.where(spot8 >= 5, near_right * right, 0.0))
+                at = base + 8 * j
+                before, after = recv[carrier, at : at + 8, :], recv[carrier, at + 24 : at + 32, :]
+                tile = jnp.where(within(5, d), roll(after, 5 - t) * right, 0.0)
+                tile = jnp.where(within(3 - d, d), roll(before, 3 - d - t) * left, tile)
                 merged.append(tile if ok is None else tile * ok)
             tiles = []
             for v in range(4):
@@ -248,17 +274,19 @@
                         store_weights(layer, c * 64 + z * 32, zp * 128, blocks[c])
                         store_weights(3 + layer, c * 64 + zp * 32, z * 128, back)
 
-    def conv(wi, bi, extent):
+    def multiply(wi, bi, lo, hi):
+        prod[bi, :, lo:hi] = jnp.dot(
+            weights[wi, :, 0:512], field[bi, :, lo:hi], preferred_element_type=F32
+        ) + jnp.dot(weights[wi, :, 512:768], field[bi, 0:256, lo:hi], preferred_element_type=F32)
+
+    def conv(wi, bi, extent, done=0):
         width = 128 * (5 + 2 * extent)
-        for lo in range(0, width, 256):
-            hi = min(lo + 256, width)
-            prod[:, lo:hi] = jnp.dot(
-                weights[wi, :, 0:512], field[bi, :, lo:hi], preferred_element_type=F32
-            ) + jnp.dot(weights[wi, :, 512:768], field[bi, 0:256, lo:hi], preferred_element_type=F32)
+        for lo in range(done, width, 256):
+            multiply(wi, bi, lo, min(lo + 256, width))
         out, edges = [], []
         for z in range(2):
             row = z * 32
-            p0, p1, p2 = (prod[c * 64 + row : c * 64 + row + 32, 512:640] for c in range(3))
+            p0, p1, p2 = (prod[bi, c * 64 + row : c * 64 + row + 32, 512:640] for c in range(3))
             edge = jnp.where(spot32 == 2, p0, roll(p2, -4))
             if extent:
                 edges.append(p1 + roll(p0, 1) + roll(p2, -1))
@@ -266,10 +294,10 @@
             for x in range(-extent, 4 + extent):
                 col = tile_of(x) * 128
                 at_edge = roll(edge, -8 * (x + 3) - 2)
-                before = roll(prod[row : row + 32, col : col + 128], 1)
-                after = roll(prod[128 + row : 160 + row, col : col + 128], -1)
+                before = roll(prod[bi, row : row + 32, col : col + 128], 1)
+                after = roll(prod[bi, 128 + row : 160 + row, col : col + 128], -1)
                 tiles[x] = (
-                    prod[64 + row : 96 + row, col : col + 128]
+                    prod[bi, 64 + row : 96 + row, col : col + 128]
                     + jnp.where(lane32 == 0, at_edge, before)
                     + jnp.where(lane32 == 127, at_edge, after)
                 )
@@ -294,7 +322,7 @@
         own = (lane32 >= 24) & (lane32 < 56)
         for z in range(2):
             for x in range(4):
-                col, at = x * 128, (z * 5 + x) * 32
+                col, at = tile_of(x) * 128, (z * 5 + x) * 32
                 tile = held[layer, at : at + 32, :]
                 store_h(0, z, col, jnp.where(lane32 == 127, 0.0, roll(tile, -1)))
                 store_h(1, z, col, tile)
@@ -323,56 +351,59 @@
         )
 
     def rs_start(layer):
-        for device, m in peers:
+        firsts, mine, count, _, _, _ = plans[layer]
+        per = 32 // count
+        for device, m in firsts:
             group_copy(
-                part.at[layer, pl.ds(m * per, per)], rs_recv.at[layer, pl.ds(me * per, per)],
+                part.at[layer, pl.ds(m * per, per)], rs_recv.at[layer, pl.ds(mine * per, per)],
                 rs_send_sem.at[layer], rs_recv_sem.at[layer], device,
             ).start()
-        rs_recv[layer, pl.ds(me * per, per)] = part[layer, pl.ds(me * per, per)]
+        rs_recv[layer, pl.ds(mine * per, per)] = part[layer, pl.ds(mine * per, per)]
 
     def rs_wait(layer):
-        count = (members - 1) * per
+        span = pl.ds(0, 32 - 32 // plans[layer][2])
         return group_copy(
-            part.at[layer, pl.ds(0, count)], rs_recv.at[layer, pl.ds(0, count)],
-            rs_send_sem.at[layer], rs_recv_sem.at[layer], near(1, 0),
+            part.at[layer, span], rs_recv.at[layer, span], rs_send_sem.at[layer], rs_recv_sem.at[layer], near(1, 0)
         )
 
     def z_start(layer):
+        _, _, count, seconds, spot, _ = plans[layer]
+        per = 32 // count
         rs_wait(layer).wait_recv()
         total = rs_recv[layer, 0:per]
-        for m in range(1, members):
+        for m in range(1, count):
             total = total + rs_recv[layer, m * per : m * per + per]
-        z_recv[layer, my_z] = total
-
-        for device in z_peers:
+        here = pl.ds(spot * per, per)
+        z_recv[layer, here] = total
+        for device in seconds:
             group_copy(
-                z_recv.at[layer, my_z], z_recv.at[layer, my_z], z_send_sem.at[layer], z_recv_sem.at[layer], device
+                z_recv.at[layer, here], z_recv.at[layer, here], z_send_sem.at[layer], z_recv_sem.at[layer], device
             ).start()
 
     def z_wait(layer):
+        span = pl.ds(0, (plans[layer][5] - 1) * (32 // plans[layer][2]))
         return group_copy(
-            z_recv.at[layer, pl.ds(0, zn - 1)], z_recv.at[layer, pl.ds(0, zn - 1)],
-            z_send_sem.at[layer], z_recv_sem.at[layer], near(1, 0),
+            z_recv.at[layer, span], z_recv.at[layer, span], z_send_sem.at[layer], z_recv_sem.at[layer], near(1, 0)
         )
 
     def ag_start(layer):
+        firsts, mine, count, _, _, others = plans[layer]
+        per = 32 // count
         z_wait(layer).wait_recv()
-        total = z_recv[layer, 0]
-        for k in range(1, zn):
-            total = total + z_recv[layer, k]
-        mine = pl.ds(me * per, per)
-        ag_recv[layer, mine] = total
-
-        for device, _ in peers:
+        total = z_recv[layer, 0:per]
+        for k in range(1, others):
+            total = total + z_recv[layer, k * per : k * per + per]
+        here = pl.ds(mine * per, per)
+        ag_recv[layer, here] = total
+        for device, _ in firsts:
             group_copy(
-                ag_recv.at[layer, mine], ag_recv.at[layer, mine], ag_send_sem.at[layer], ag_recv_sem.at[layer], device
+                ag_recv.at[layer, here], ag_recv.at[layer, here], ag_send_sem.at[layer], ag_recv_sem.at[layer], device
             ).start()
 
     def ag_wait(layer):
-        count = pl.ds(0, (members - 1) * per)
+        span = pl.ds(0, 32 - 32 // plans[layer][2])
         return group_copy(
-            ag_recv.at[layer, count], ag_recv.at[layer, count],
-            ag_send_sem.at[layer], ag_recv_sem.at[layer], near(1, 0),
+            ag_recv.at[layer, span], ag_recv.at[layer, span], ag_send_sem.at[layer], ag_recv_sem.at[layer], near(1, 0)
         )
 
     def finish(layer):
@@ -381,25 +412,31 @@
 
     def sequence():
         loads[0].wait()
-        tiles3 = load_tiles(x3)
-        packed3 = edge_columns(tiles3)
-        fill_send(0, tiles3, packed3)
+        loads[4].wait()
+        tiles3, tiles1 = load_tiles(x3), load_tiles(x1)
+        fill_columns(0, {0: edge_columns(tiles3), 3: edge_columns(tiles1)})
+        fill_send(0, tiles3)
         pl.semaphore_wait(barrier, len(greeted))
         start_halo(0)
+        loads[2].wait()
+        loads[3].wait()
+        tiles, tiles2 = load_tiles(cot), load_tiles(x2)
+        fill_columns(1, {1: edge_columns(tiles), 2: edge_columns(tiles2)})
+        fill_send(1, tiles)
+        start_halo(1)
+        fill_send(2, tiles2)
+        start_halo(2)
+        fill_send(3, tiles1)
+        start_halo(3)
         zero = [zero32, zero32]
-        for f, ref, at in ((1, cot, 2), (2, x2, 3), (3, x1, 4)):
-            loads[at].wait()
-            tiles = load_tiles(ref)
-            packed = edge_columns(tiles)
-            fill_send(f, tiles, packed)
-            start_halo(f)
-            if f > 1:
-                fill_rows(f - 1, 3 - f, tiles)
+        fill_rows(1, 1, tiles2)
+        fill_rows(2, 0, tiles1)
         clear_padding()
         fill_rows(0, 2, tiles3)
         for at, kernel, layer in ((1, k3, 0), (5, k2, 1), (6, k1, 2)):
             loads[at].wait()
             build_weights(layer, kernel)
+            multiply(layer, layer, 0, 256)
 
         def forward(layer, f, extent, ref):
             near_packed = edge_columns(load_tiles(ref)) if extent else zero
@@ -410,7 +447,7 @@
                 far_packed = edge_columns(rows)
                 edges = own_edges([near_packed[z] + far_packed[z] for z in range(2)], edges)
             fill_edges(layer, edges)
-            return conv(layer, layer, extent)
+            return conv(layer, layer, extent, 256)
 
         pre, pre_edge = forward(0, 0, 2, x3)
         whole_halo(1).wait_recv()
@@ -441,7 +478,8 @@
         pre, _ = forward(2, 3, 0, x1)
         h = [{x: grad[z][x] * gelu_slope(pre[z][x]) for x in range(4)} for z in range(2)]
         packed = edge_columns(h)
-        fill_send(4, h, packed)
+        fill_columns(4, {4: packed})
+        fill_send(4, h)
         start_halo(4)
         keep_h(2, h, packed)
         kernel_grad(2)
@@ -451,6 +489,7 @@
         kernel_grad(1)
         rs_start(1)
         fill_rows(5, 0, h)
+        z_start(2)
         whole_halo(4).wait_recv()
         fill_rows(5, 0, halo_rows(4))
         fill_edges(5, halo_edges(4))
@@ -458,7 +497,6 @@
         for z in range(2):
             for x in range(4):
                 gin_ref[pl.ds(z * 4 + x, 32, stride=8), :] = grad[z][x]
-        z_start(2)
         z_start(0)
         z_start(1)
         ag_start(2)
@@ -499,7 +537,7 @@
     vmem = pl.BlockSpec(memory_space=pltpu.VMEM)
     hbm = pl.BlockSpec(memory_space=pltpu.HBM)
     members = dims[3] * 2 * dims[1]
-    per = 32 // members
+    rows = max(dims[2] * (32 // members), members // 2 * (16 // dims[2]))
     dma = pltpu.SemaphoreType.DMA
     gin, red = pl.pallas_call(
         functools.partial(step_kernel, dims),
@@ -514,11 +552,11 @@
             pltpu.VMEM((6, 512, 1152), BF16),
             pltpu.VMEM((6, 192, 768), BF16),
             pltpu.VMEM((384, 640), BF16),
-            pltpu.VMEM((192, 1152), F32),
+            pltpu.VMEM((6, 192, 1152), F32),
             pltpu.VMEM((3, 320, 128), F32),
             pltpu.VMEM((3, 32, 8, 128), F32),
             pltpu.VMEM((3, 32, 8, 128), F32),
-            pltpu.VMEM((3, dims[2], per, 8, 128), F32),
+            pltpu.VMEM((3, rows, 8, 128), F32),
             pltpu.VMEM((3, 32, 8, 128), F32),
             dma((7,)), dma((5,)), dma((5,)), dma((3,)), dma((3,)), dma((3,)), dma((3,)), dma((3,)), dma((3,)),
         ],

time: 41.2 us -> 39.9 us (0.968)
  Pallas kernels: 40.4 us -> 39.1 us
    pallas_call x1, Pallas kernels: 39.1 us -> 37.8 us  [per_device(): pl.pallas_call(functools.partial(step_kernel, dims), out_shape=(jax.Shape...]
where the time goes in v5:
time: 39.9 us; the launch traced here: 39.7 us
  Pallas kernels  39.1 us (98%)
  between operations  0.64 us (2%)
    pallas_call x1, Pallas kernels, per_device(): pl.pallas_call(functools.partial(step_kernel, dims), out_shape=(jax.Shape...  37.8 us
    pallas_call x1, Pallas kernels, per_device(): pl.pallas_call(functools.partial(unpack_kernel, factor), out_shape=(jax.S...  1.33 us

profile of v5, /device:TPU:1, one launch (start us, length us, event | category | flops | bytes accessed | tf_op | source)
XLA Modules:
  0.0 39.7 jit_solution(3193085669571122503)
XLA Ops:
  0.6 37.8 %step.1 = (f32[256,128]{1,0:T(8,128)S(1)}, f32[3,32,8,128]{3,2,1,0:T(8,128)S(1)}) custom-call(f32[256,128]{1,0:T(8,128)} %bitcast.7, f32[256,128]{1,0:T(8,128)} %bitcast.8, f32[256,128]{1,0:T(8,128)} %bitcast.9, f32[256,128]{1,0:T(8,128)} %bitcast.10, f32[27,32,32]{2,1,0:T(8,128)} %k3_in.1, f32[27,32,32]{2,1,0:T(8,128)} %k2_in.1, f32[27,32,32]{2,1,0:T(8,128)} %k1_in.1), custom_call_target="tpu_custom_call" | custom-call | tf_op jit(solution)/shard_map/step/pallas_call | solution.py:542
  38.4 1.3 %unpack.1 = (f32[256,128]{1,0:T(8,128)}, f32[27,32,32]{2,1,0:T(8,128)}, f32[27,32,32]{2,1,0:T(8,128)}, f32[27,32,32]{2,1,0:T(8,128)}) custom-call(f32[256,128]{1,0:T(8,128)S(1)} %get-tuple-element.10.gin_in, f32[3,256,128]{2,1,0:T(8,128)S(1)} %bitcast.6), custom_call_target="tpu_custom_call" | custom-call | tf_op jit(solution)/shard_map/unpack/pallas_call | solution.py:569

commit v6 on v5

--- a/solution.py
+++ b/solution.py
@@ -46,7 +46,7 @@
     x3, cot, x2, x1, k3, k2, k1,
     send, recv, field, weights, hmat, prod, held,
     part, rs_recv, z_recv, ag_recv,
-    load_sem, halo_send, halo_recv, rs_send_sem, rs_recv_sem, z_send_sem, z_recv_sem, ag_send_sem, ag_recv_sem,
+    load_sem, halo_send, halo_recv, pack_recv, rs_send_sem, rs_recv_sem, z_send_sem, z_recv_sem, ag_send_sem, ag_recv_sem,
 ):
     gxn, gyn, zn, ylo = dims
     members = ylo * 2 * gyn
@@ -190,21 +190,21 @@
     def start_halo(f):
         d = depth[f] * 64
 
-        def go(src, dst, rows, device):
+        def go(src, dst, rows, device, arrival):
             pltpu.make_async_remote_copy(
                 src_ref=send.at[f, pl.ds(src, rows)],
                 dst_ref=recv.at[f, pl.ds(dst, rows)],
                 send_sem=halo_send.at[f],
-                recv_sem=halo_recv.at[f],
+                recv_sem=arrival.at[f],
                 device_id=device,
                 device_id_type=MESH,
             ).start()
 
         if f in riders:
             for k in (0, 2, 3, 5, 1, 4):
-                go(256 if k < 3 else 264, 2 * d + 8 * k, 8, near(-SIDES[k][0], -SIDES[k][1]))
-        go(256 - d, 0, d, near(1, 0))
-        go(0, d, d, near(-1, 0))
+                go(256 if k < 3 else 264, 2 * d + 8 * k, 8, near(-SIDES[k][0], -SIDES[k][1]), pack_recv)
+        go(256 - d, 0, d, near(1, 0), halo_recv)
+        go(0, d, d, near(-1, 0), halo_recv)
 
     def whole_halo(f):
         ref = recv.at[f, pl.ds(0, 128 * depth[f] + (48 if f in riders else 0))]
@@ -212,6 +212,20 @@
             src_ref=ref, dst_ref=ref, send_sem=halo_send.at[f], recv_sem=halo_recv.at[f],
             device_id=near(1, 0), device_id_type=MESH,
         )
+
+    def wait_rows(f):
+        ref = recv.at[f, pl.ds(0, 128 * depth[f])]
+        pltpu.make_async_remote_copy(
+            src_ref=ref, dst_ref=ref, send_sem=halo_send.at[f], recv_sem=halo_recv.at[f],
+            device_id=near(1, 0), device_id_type=MESH,
+        ).wait_recv()
+
+    def wait_columns(f):
+        ref = recv.at[f, pl.ds(128 * depth[f], 48)]
+        pltpu.make_async_remote_copy(
+            src_ref=ref, dst_ref=ref, send_sem=halo_send.at[f], recv_sem=pack_recv.at[f],
+            device_id=near(1, 0), device_id_type=MESH,
+        ).wait_recv()
 
     def halo_rows(f):
         d = depth[f]
@@ -279,10 +293,10 @@
             weights[wi, :, 0:512], field[bi, :, lo:hi], preferred_element_type=F32
         ) + jnp.dot(weights[wi, :, 512:768], field[bi, 0:256, lo:hi], preferred_element_type=F32)
 
-    def conv(wi, bi, extent, done=0):
+    def conv(wi, bi, extent, chunks=None):
         width = 128 * (5 + 2 * extent)
-        for lo in range(done, width, 256):
-            multiply(wi, bi, lo, min(lo + 256, width))
+        for lo, hi in chunks or [(lo, min(lo + 256, width)) for lo in range(0, width, 256)]:
+            multiply(wi, bi, lo, hi)
         out, edges = [], []
         for z in range(2):
             row = z * 32
@@ -440,17 +454,24 @@
 
         def forward(layer, f, extent, ref):
             near_packed = edge_columns(load_tiles(ref)) if extent else zero
-            whole_halo(f).wait_recv()
-            rows, edges = halo_rows(f), halo_edges(f)
+            wait_rows(f)
+            rows = halo_rows(f)
             fill_rows(layer, extent, rows)
+            multiply(layer, layer, 256, 512)
+            for lo in range(640, 640 + 256 * extent, 256):
+                multiply(layer, layer, lo, lo + 256)
+            if f == 0:
+                wait_columns(0)
+            edges = halo_edges(f)
             if extent:
                 far_packed = edge_columns(rows)
                 edges = own_edges([near_packed[z] + far_packed[z] for z in range(2)], edges)
             fill_edges(layer, edges)
-            return conv(layer, layer, extent, 256)
+            return conv(layer, layer, extent, ((512, 640),))
 
         pre, pre_edge = forward(0, 0, 2, x3)
-        whole_halo(1).wait_recv()
+        wait_rows(1)
+        wait_columns(1)
         grad, far = load_tiles(cot), halo_rows(1)
         h = []
         for z in range(2):
@@ -490,15 +511,16 @@
         rs_start(1)
         fill_rows(5, 0, h)
         z_start(2)
-        whole_halo(4).wait_recv()
+        z_start(0)
+        z_start(1)
+        wait_rows(4)
+        wait_columns(4)
         fill_rows(5, 0, halo_rows(4))
         fill_edges(5, halo_edges(4))
         grad, _ = conv(5, 5, 0)
         for z in range(2):
             for x in range(4):
                 gin_ref[pl.ds(z * 4 + x, 32, stride=8), :] = grad[z][x]
-        z_start(0)
-        z_start(1)
         ag_start(2)
         ag_start(0)
         ag_start(1)
@@ -558,7 +580,7 @@
             pltpu.VMEM((3, 32, 8, 128), F32),
             pltpu.VMEM((3, rows, 8, 128), F32),
             pltpu.VMEM((3, 32, 8, 128), F32),
-            dma((7,)), dma((5,)), dma((5,)), dma((3,)), dma((3,)), dma((3,)), dma((3,)), dma((3,)), dma((3,)),
+            dma((7,)), dma((5,)), dma((5,)), dma((5,)), dma((3,)), dma((3,)), dma((3,)), dma((3,)), dma((3,)), dma((3,)),
         ],
         compiler_params=pltpu.CompilerParams(
             collective_id=0, has_side_effects=True, vmem_limit_bytes=40 * 1024 * 1024

time: 39.9 us -> 39.9 us (level)
  no operation moved by 1% of the time
where the time goes in v6:
time: 39.9 us; the launch traced here: 39.8 us
  Pallas kernels  39.1 us (98%)
  between operations  0.64 us (2%)
    pallas_call x1, Pallas kernels, per_device(): pl.pallas_call(functools.partial(step_kernel, dims), out_shape=(jax.Shape...  37.8 us
    pallas_call x1, Pallas kernels, per_device(): pl.pallas_call(functools.partial(unpack_kernel, factor), out_shape=(jax.S...  1.33 us

profile of v6, /device:TPU:1, one launch (start us, length us, event | category | flops | bytes accessed | tf_op | source)
XLA Modules:
  0.0 39.8 jit_solution(15791755758820689429)
XLA Ops:
  0.6 37.8 %step.1 = (f32[256,128]{1,0:T(8,128)S(1)}, f32[3,32,8,128]{3,2,1,0:T(8,128)S(1)}) custom-call(f32[256,128]{1,0:T(8,128)} %bitcast.7, f32[256,128]{1,0:T(8,128)} %bitcast.8, f32[256,128]{1,0:T(8,128)} %bitcast.9, f32[256,128]{1,0:T(8,128)} %bitcast.10, f32[27,32,32]{2,1,0:T(8,128)} %k3_in.1, f32[27,32,32]{2,1,0:T(8,128)} %k2_in.1, f32[27,32,32]{2,1,0:T(8,128)} %k1_in.1), custom_call_target="tpu_custom_call" | custom-call | tf_op jit(solution)/shard_map/step/pallas_call | solution.py:564
  38.4 1.3 %unpack.1 = (f32[256,128]{1,0:T(8,128)}, f32[27,32,32]{2,1,0:T(8,128)}, f32[27,32,32]{2,1,0:T(8,128)}, f32[27,32,32]{2,1,0:T(8,128)}) custom-call(f32[256,128]{1,0:T(8,128)S(1)} %get-tuple-element.10.gin_in, f32[3,256,128]{2,1,0:T(8,128)S(1)} %bitcast.6), custom_call_target="tpu_custom_call" | custom-call | tf_op jit(solution)/shard_map/unpack/pallas_call | solution.py:591
